TPU v7x, 32 devices: a whole 2x2x4 slice. The times are simulated.
32 devices in a mesh: gy: 8 (over z, x), gz: 4 (over y, core).
Axes of the slice: x: 2, y: 2, z: 4, core: 2. Of those that a mesh axis runs over, the one named last changes fastest.
Arguments:
- tokens: bfloat16 [16, 64, 16, 192], P(None, 'gy', 'gz'), may hold values from -36 to 36
- qkv_weight: bfloat16 [192, 576], replicated, may hold values from -0.4375 to 0.4375
- out_weight: bfloat16 [192, 192], replicated, may hold values from -1.25 to 1.25
- conv_kernel: float32 [3, 3, 3, 192], replicated, may hold values from -1.25 to 1.25
- up_weight: bfloat16 [192, 768], replicated, may hold values from -0.4375 to 0.4375
- down_weight: bfloat16 [768, 192], replicated, may hold values from -0.21875 to 0.21875
- band_mask: int32 [4, 4], replicated, may hold values from 0 to 1, as said below
- grad_out: bfloat16 [16, 64, 16, 192], P(None, 'gy', 'gz'), may hold values from -6 to 6
Outputs:
- block_out: bfloat16 [16, 64, 16, 192], P(None, 'gy', 'gz')
- token_gradient: bfloat16 [16, 64, 16, 192], P(None, 'gy', 'gz')
- qkv_gradient: float32 [192, 576], replicated
- out_gradient: float32 [192, 192], replicated
- kernel_gradient: float32 [3, 3, 3, 192], replicated
- up_gradient: float32 [192, 768], replicated
- down_gradient: float32 [768, 192], replicated
Inputs may be any that keep to these rules, and one draw needn't show every extreme that they name: band_mask[i, i] is 1, and band_mask[i, j] is 0 where |i - j| > 4; other entries are 0 or 1.
All inputs are finite; a program needn't handle non-finite values.
Results may differ from a plain program's by a relative error of at most 0.017.
Values may be sent and summed in bfloat16 or wider, within the bound.
A program may use at most 64 MiB of HBM per device.

v0:
```python
import math

import jax
import jax.numpy as jnp
from jax import lax
from jax.sharding import PartitionSpec as P

HEADS = 6
BLOCK = 16


NORM_EPS = 1e-05
UNIT_EPS = 1e-06
GELU_SLOPE = 0.7978845608028654
GELU_CUBIC = 0.044715


def with_halo(cells, sides, width):
    for axis, dim in sides:
        count = lax.axis_size(axis)
        head = lax.slice_in_dim(cells, 0, width, axis=dim)
        tail = lax.slice_in_dim(cells, cells.shape[dim] - width, cells.shape[dim], axis=dim)
        cells = jnp.concatenate(
            [
                lax.ppermute(tail, axis, [(i, (i + 1) % count) for i in range(count)]),
                cells,
                lax.ppermute(head, axis, [((i + 1) % count, i) for i in range(count)]),
            ],
            axis=dim,
        )
    return cells


def norm_rows(values):
    centred = values - jnp.mean(values, axis=-1, keepdims=True)
    inverse = lax.rsqrt(jnp.mean(centred * centred, axis=-1, keepdims=True) + NORM_EPS)
    return (centred * inverse, inverse)


def norm_rows_back(upstream, normal, inverse):
    return inverse * (
        upstream
        - jnp.mean(upstream, axis=-1, keepdims=True)
        - normal * jnp.mean(upstream * normal, axis=-1, keepdims=True)
    )


def unit_scale(values):
    return lax.rsqrt(jnp.mean(values * values, axis=-1, keepdims=True) + UNIT_EPS)


def unit_back(upstream, values, scaling):
    return scaling * upstream - scaling * scaling * scaling * values * jnp.mean(
        upstream * values, axis=-1, keepdims=True
    )


def gelu_value(pre_act):
    return (
        0.5
        * pre_act
        * (1.0 + jnp.tanh(GELU_SLOPE * (pre_act + GELU_CUBIC * pre_act * pre_act * pre_act)))
    )


def gelu_slope(pre_act):
    tangent = jnp.tanh(GELU_SLOPE * (pre_act + GELU_CUBIC * pre_act * pre_act * pre_act))
    return 0.5 * (1.0 + tangent) + 0.5 * pre_act * (1.0 - tangent * tangent) * GELU_SLOPE * (
        1.0 + 3.0 * GELU_CUBIC * pre_act * pre_act
    )


def flatten_rows(values):
    return values.reshape(-1, values.shape[-1])


def project(values, weight):
    summed = jnp.dot(flatten_rows(values), weight, preferred_element_type=jnp.float32)
    return summed.reshape(values.shape[:-1] + (weight.shape[1],))


def project_back(values, weight):
    summed = lax.dot_general(
        flatten_rows(values), weight, (((1,), (1,)), ((), ())), preferred_element_type=jnp.float32
    )
    return summed.reshape(values.shape[:-1] + (weight.shape[0],))


def contract(left_rows, right_rows):
    return lax.dot_general(
        flatten_rows(left_rows),
        flatten_rows(right_rows),
        (((0,), (0,)), ((), ())),
        preferred_element_type=jnp.float32,
    )


def split_heads(values, head_count):
    return values.reshape(values.shape[:-1] + (head_count, values.shape[-1] // head_count))


def join_heads(values):
    return values.reshape(values.shape[:-2] + (values.shape[-2] * values.shape[-1],))


def head_product(einsum_form, left_side, right_side):
    return jnp.einsum(einsum_form, left_side, right_side, preferred_element_type=jnp.float32)


def attention_parts(qkv_rows, mask_full, head_count):
    feature_width = qkv_rows.shape[-1] // 3
    query_vec = qkv_rows[..., :feature_width].astype(jnp.float32)
    key_vec = qkv_rows[..., feature_width : 2 * feature_width].astype(jnp.float32)
    query_scale = unit_scale(query_vec)
    key_scale = unit_scale(key_vec)
    query_unit = (query_vec * query_scale).astype(jnp.bfloat16)
    key_unit = (key_vec * key_scale).astype(jnp.bfloat16)
    factor = 2.0 / math.sqrt(feature_width // head_count)
    scores = head_product(
        "aibhd,ajbhd->abhij", split_heads(query_unit, head_count), split_heads(key_unit, head_count)
    )
    weights = mask_full * jnp.exp(factor * scores)
    attn_probs = weights / jnp.sum(weights, axis=-1, keepdims=True)
    return (query_vec, key_vec, query_scale, key_scale, query_unit, key_unit, attn_probs, factor)


def attend(qkv_rows, mask_full, head_count):
    query_vec, key_vec, query_scale, key_scale, query_unit, key_unit, attn_probs, factor = (
        attention_parts(qkv_rows, mask_full, head_count)
    )
    feature_width = qkv_rows.shape[-1] // 3
    value_heads = split_heads(qkv_rows[..., 2 * feature_width :], head_count)
    probs_low = attn_probs.astype(jnp.bfloat16)
    mixed_heads = head_product("abhij,ajbhd->aibhd", probs_low, value_heads)
    return join_heads(mixed_heads).astype(jnp.bfloat16)


def attend_back(qkv_rows, mask_full, head_count, upstream):
    query_vec, key_vec, query_scale, key_scale, query_unit, key_unit, attn_probs, factor = (
        attention_parts(qkv_rows, mask_full, head_count)
    )
    feature_width = qkv_rows.shape[-1] // 3
    value_heads = split_heads(qkv_rows[..., 2 * feature_width :], head_count)
    grad_heads = split_heads(upstream, head_count)
    probs_low = attn_probs.astype(jnp.bfloat16)
    grad_probs = head_product("aibhd,ajbhd->abhij", grad_heads, value_heads)
    grad_values = head_product("abhij,aibhd->ajbhd", probs_low, grad_heads)
    grad_scores = attn_probs * (
        grad_probs - jnp.sum(grad_probs * attn_probs, axis=-1, keepdims=True)
    )
    grad_low = (factor * grad_scores).astype(jnp.bfloat16)
    grad_qunit = join_heads(
        head_product("abhij,ajbhd->aibhd", grad_low, split_heads(key_unit, head_count))
    )
    grad_kunit = join_heads(
        head_product("abhij,aibhd->ajbhd", grad_low, split_heads(query_unit, head_count))
    )
    grad_query = unit_back(grad_qunit, query_vec, query_scale).astype(jnp.bfloat16)
    grad_key = unit_back(grad_kunit, key_vec, key_scale).astype(jnp.bfloat16)
    return jnp.concatenate(
        [grad_query, grad_key, join_heads(grad_values).astype(jnp.bfloat16)], axis=-1
    )


def conv_apply(padded, kernel_taps):
    extent_x = padded.shape[0] - 2
    extent_y = padded.shape[1] - 2
    extent_z = padded.shape[2] - 2
    summed = jnp.zeros((extent_x, extent_y, extent_z, padded.shape[3]), jnp.float32)
    for shift_x in range(3):
        for shift_y in range(3):
            for shift_z in range(3):
                window = padded[
                    shift_x : shift_x + extent_x,
                    shift_y : shift_y + extent_y,
                    shift_z : shift_z + extent_z,
                ]
                summed = summed + kernel_taps[shift_x, shift_y, shift_z] * window.astype(
                    jnp.float32
                )
    return summed


def kernel_grad(padded, upstream):
    extent_x, extent_y, extent_z, channels = upstream.shape
    upstream_wide = upstream.astype(jnp.float32)
    pieces = []
    for shift_x in range(3):
        for shift_y in range(3):
            for shift_z in range(3):
                window = padded[
                    shift_x : shift_x + extent_x,
                    shift_y : shift_y + extent_y,
                    shift_z : shift_z + extent_z,
                ]
                pieces.append(jnp.sum(window.astype(jnp.float32) * upstream_wide, axis=(0, 1, 2)))
    return jnp.stack(pieces).reshape(3, 3, 3, channels)


def mlp_pass(mixed_field, upstream, up_weight, down_weight):
    mixed_wide = mixed_field.astype(jnp.float32)
    normal, inverse = norm_rows(mixed_wide)
    normed = normal.astype(jnp.bfloat16)
    pre_act = project(normed, up_weight)
    hidden = gelu_value(pre_act).astype(jnp.bfloat16)
    block_out = (mixed_wide + project(hidden, down_weight)).astype(jnp.bfloat16)
    grad_hidden = project_back(upstream, down_weight).astype(jnp.bfloat16)
    part_down = contract(hidden, upstream)
    grad_pre = (grad_hidden.astype(jnp.float32) * gelu_slope(pre_act)).astype(jnp.bfloat16)
    part_up = contract(normed, grad_pre)
    grad_normed = project_back(grad_pre, up_weight)
    grad_mixed = (
        upstream.astype(jnp.float32) + norm_rows_back(grad_normed, normal, inverse)
    ).astype(jnp.bfloat16)
    return (block_out, grad_mixed, part_up, part_down)


def attention_exchange_back(qkv_lines, mask_full):
    return lax.all_to_all(
        attend(qkv_lines, mask_full, HEADS), "gy", split_axis=1, concat_axis=0, tiled=True
    )


def extend_values(field_values):
    grown = with_halo(field_values, (("gy", 1), ("gz", 2)), 1)
    return jnp.pad(grown, ((1, 1), (0, 0), (0, 0), (0, 0)))


def extend_grads(field_values):
    grown = with_halo(field_values, (("gy", 1), ("gz", 2)), 1)
    return jnp.pad(grown, ((1, 1), (0, 0), (0, 0), (0, 0)))


def local(tokens, qkv_weight, out_weight, conv_kernel, up_weight, down_weight, band_mask, grad_out):
    block_count = band_mask.shape[0]
    line_length = block_count * BLOCK
    mask_full = (
        jnp.broadcast_to(band_mask[:, None, :, None], (block_count, BLOCK, block_count, BLOCK))
        .reshape(line_length, line_length)
        .astype(jnp.float32)
    )
    flipped = conv_kernel[::-1, ::-1, ::-1]
    token_wide = tokens.astype(jnp.float32)
    normal_first, inverse_first = norm_rows(token_wide)
    normed_first = normal_first.astype(jnp.bfloat16)
    qkv_rows = project(normed_first, qkv_weight).astype(jnp.bfloat16)
    line_items = lax.all_to_all(qkv_rows, "gy", split_axis=0, concat_axis=1, tiled=True)
    attended = attention_exchange_back(line_items, mask_full)
    value_field = (token_wide + project(attended, out_weight)).astype(jnp.bfloat16)
    padded_value = extend_values(value_field)
    mixed_field = (value_field.astype(jnp.float32) + conv_apply(padded_value, conv_kernel)).astype(
        jnp.bfloat16
    )
    block_out, grad_mixed, part_up, part_down = mlp_pass(
        mixed_field, grad_out, up_weight, down_weight
    )
    padded_grad = extend_grads(grad_mixed)
    grad_value = (grad_mixed.astype(jnp.float32) + conv_apply(padded_grad, flipped)).astype(
        jnp.bfloat16
    )
    part_kernel = kernel_grad(padded_value, grad_mixed)
    grad_attended = project_back(grad_value, out_weight).astype(jnp.bfloat16)
    part_out = contract(attended, grad_value)
    grad_lines = lax.all_to_all(grad_attended, "gy", split_axis=0, concat_axis=1, tiled=True)
    grad_qkv_lines = attend_back(line_items, mask_full, HEADS, grad_lines)
    grad_qkv_rows = lax.all_to_all(grad_qkv_lines, "gy", split_axis=1, concat_axis=0, tiled=True)
    grad_normed = project_back(grad_qkv_rows, qkv_weight).astype(jnp.bfloat16)
    part_qkv = contract(normed_first, grad_qkv_rows)
    token_gradient = (
        grad_value.astype(jnp.float32)
        + norm_rows_back(grad_normed.astype(jnp.float32), normal_first, inverse_first)
    ).astype(jnp.bfloat16)
    summed_parts = lax.psum((part_qkv, part_out, part_kernel, part_up, part_down), ("gy", "gz"))
    token_count = (
        tokens.shape[0]
        * tokens.shape[1]
        * lax.axis_size("gy")
        * tokens.shape[2]
        * lax.axis_size("gz")
    )
    factor = 1.0 / math.sqrt(token_count)
    return (
        block_out,
        token_gradient,
        summed_parts[0] * factor,
        summed_parts[1] * factor,
        summed_parts[2] * factor,
        summed_parts[3] * factor,
        summed_parts[4] * factor,
    )


def solution(mesh):
    placed = (P(None, "gy", "gz", None), P(), P(), P(), P(), P(), P(), P(None, "gy", "gz", None))
    return jax.shard_map(
        local,
        mesh=mesh,
        in_specs=placed,
        out_specs=(P(None, "gy", "gz", None), P(None, "gy", "gz", None), P(), P(), P(), P(), P()),
        check_vma=False,
    )
```

profile of v0, /device:TPU:0, one launch (start us, length us, event | category | flops | bytes accessed | tf_op | source)
XLA Modules:
  0.0 343.9 jit_solution(10555786560866475854)
XLA Ops:
  10.8 2.1 convolution_convert_fusion.1
  12.9 7.3 %all-to-all-start = ((bf16[16,8,4,576]{3,1,2,0:T(8,128)(2,1)}), bf16[16,8,4,576]{3,1,2,0:T(8,128)(2,1)S(1)}, u32[]{:S(2)}, u32[]{:S(2)}) async-start(bf16[16,8,4,576]{3,1,2,0:T(8,128)(2,1)} %convolution_convert_fusion.1), calls=%async_computation | async-start | bytes 1310720 | tf_op jit(solution)/shard_map/all_to_all | solution.py:247
  20.5 17.0 %all-to-all-done = bf16[16,8,4,576]{3,1,2,0:T(8,128)(2,1)S(1)} async-done(((bf16[16,8,4,576]{3,1,2,0:T(8,128)(2,1)}), bf16[16,8,4,576]{3,1,2,0:T(8,128)(2,1)S(1)}, u32[]{:S(2)}, u32[]{:S(2)}) %all-to-all-start) | async-done | bytes 589856 | tf_op jit(solution)/shard_map/all_to_all | solution.py:247
  42.6 2.4 convolution_convert_fusion.3
  46.3 12.5 %all_to_all.63 = bf16[2,64,4,192]{3,2,0,1:T(4,128)(2,1)S(1)} all-to-all(bf16[2,64,4,192]{3,2,0,1:T(4,128)(2,1)S(1)} %copy.104), channel_id=1, replica_groups=mesh['gy'=8,'gz'=4] {'gy'}, dimensions={1} | all-to-all | bytes 393216 | tf_op jit(solution)/shard_map/all_to_all | solution.py:219
  60.8 3.3 collective-permute-start.1
  66.5 1.7 collective-permute-start.3
  72.8 2.4 convert_reduce_fusion
  78.3 1.8 fusion.121
  81.5 4.0 %collective-permute-start.5 = (bf16[16,1,4,192]{3,1,2,0:T(2,128)(2,1)}, bf16[16,1,4,192]{3,1,2,0:T(2,128)(2,1)S(1)}, u32[]{:S(2)}, u32[]{:S(2)}) collective-permute-start(bf16[16,1,4,192]{3,1,2,0:T(2,128)(2,1)} %get-tuple-element.96), channel_id=1, source_target_pairs={{4,0},{8,4},{12,8},{16,12},{20,16},{24,20},{28,24},{0,28},{5,1},{9... | collective-permute-start | bytes 73736 | tf_op jit(solution)/shard_map/ppermute | solution.py:27
  90.2 1.8 fusion.130
  95.2 2.2 fusion.132
  98.4 5.7 %all-to-all-start.2 = ((bf16[16,8,4,192]{3,1,2,0:T(8,128)(2,1)}), bf16[16,8,4,192]{3,1,2,0:T(8,128)(2,1)}, u32[]{:S(2)}, u32[]{:S(2)}) async-start(bf16[16,8,4,192]{3,1,2,0:T(8,128)(2,1)} %convolution_convert_fusion.4), calls=%async_computation.2 | async-start | bytes 524288 | tf_op jit(solution)/shard_map/all_to_all | solution.py:264
  104.2 2.2 fusion.18
  107.4 2.8 stack.111
  110.2 41.6 %psum.37 = f32[3,3,3,192]{3,2,1,0:T(4,128)S(1)} all-reduce(f32[3,3,3,192]{3,2,1,0:T(4,128)S(1)} %reshape.191), channel_id=1, replica_groups=mesh['gy'=8,'gz'=4] {'gy','gz'}, use_global_device_ids=true, to_apply=%region_43.44 | all-reduce | flops 5184 | bytes 41472 | tf_op jit(solution)/shard_map/psum | solution.py:273
  151.8 2.5 convolution_bitcast_fusion.1
  157.0 3.2 convolution_convert_fusion.2
  161.8 3.3 fusion.16
  165.1 3.4 %fusion.13 = f32[2,4,6,32,64]{4,3,2,1,0:T(8,128)} fusion(bf16[2,64,4,6,32]{1,4,3,2,0:T(8,128)(2,1)} %bitcast.173, f32[2,4,6,64,64]{3,4,2,1,0:T(8,128)} %fusion.27, f32[2,4,6,64,64]{3,4,2,1,0:T(8,128)S(1)} %fusion.163), kind=kOutput, calls=%fused_computation.47 | convolution fusion | flops 13569087 | bytes 2162688 | tf_op jit(solution)/shard_map/abhij,aibhd->ajbhd/dot_general | solution.py:107
  175.2 5.2 %all-to-all-start.3 = ((bf16[2,64,4,576]{3,2,0,1:T(4,128)(2,1)}), bf16[2,64,4,576]{3,2,0,1:T(4,128)(2,1)S(1)}, u32[]{:S(2)}, u32[]{:S(2)}) async-start(bf16[2,64,4,576]{3,2,0,1:T(4,128)(2,1)} %copy.120), calls=%async_computation.3 | async-start | bytes 1310720 | tf_op jit(solution)/shard_map/all_to_all | solution.py:266
  183.7 12.4 %all-to-all-done.3 = bf16[2,64,4,576]{3,2,0,1:T(4,128)(2,1)S(1)} async-done(((bf16[2,64,4,576]{3,2,0,1:T(4,128)(2,1)}), bf16[2,64,4,576]{3,2,0,1:T(4,128)(2,1)S(1)}, u32[]{:S(2)}, u32[]{:S(2)}) %all-to-all-start.3) | async-done | bytes 589856 | tf_op jit(solution)/shard_map/all_to_all | solution.py:266
  200.5 131.3 %all-reduce.5.cloned.1.call-done = (f32[192,576]{1,0:T(8,128)}, f32[192,192]{1,0:T(8,128)}, f32[192,768]{1,0:T(8,128)}, f32[768,192]{0,1:T(8,128)}) async-done(((f32[192,576]{1,0:T(8,128)}, f32[192,192]{1,0:T(8,128)}, f32[192,768]{1,0:T(8,128)}, f32[768,192]{0,1:T(8,128)}), (f32[192,576]{1,0:T(8,128)}, f32[192,192]{1,0:T(8,128)}, f32[192,768]{1,0:T(8,128)}, ...) | async-done | bytes 1769488 | tf_op jit(solution)/shard_map/psum | solution.py:273
  331.8 1.9 broadcast_multiply_fusion.2
  (273 shorter events, 54.3 us)
Async XLA Ops:
  7.2 68.4 %copy-start = (bf16[192,768]{1,0:T(8,128)(2,1)S(1)}, bf16[192,768]{1,0:T(8,128)(2,1)}, u32[]{:S(2)}) copy-start(bf16[192,768]{1,0:T(8,128)(2,1)} %param.12) | copy-start | bytes 884740
  9.6 10.6 %copy-start.85 = (s32[4,4]{1,0:T(4,128)S(1)}, s32[4,4]{1,0:T(4,128)}, u32[]{:S(2)}) copy-start(s32[4,4]{1,0:T(4,128)} %param.14) | copy-start | bytes 196
  12.9 24.5 %all-to-all-start = ((bf16[16,8,4,576]{3,1,2,0:T(8,128)(2,1)}), bf16[16,8,4,576]{3,1,2,0:T(8,128)(2,1)S(1)}, u32[]{:S(2)}, u32[]{:S(2)}) async-start(bf16[16,8,4,576]{3,1,2,0:T(8,128)(2,1)} %convolution_convert_fusion.1), calls=%async_computation | async-start | bytes 1310720 | tf_op jit(solution)/shard_map/all_to_all | solution.py:247
  45.0 13.9 %copy-start.1 = (bf16[16,8,4,192]{3,2,1,0:T(4,128)(2,1)S(1)}, bf16[16,8,4,192]{3,2,1,0:T(4,128)(2,1)}, u32[]{:S(2)}) copy-start(bf16[16,8,4,192]{3,2,1,0:T(4,128)(2,1)} %param.8) | copy-start | bytes 589828
  45.0 13.9 %copy-start.11 = (bf16[192,192]{1,0:T(8,128)(2,1)S(1)}, bf16[192,192]{1,0:T(8,128)(2,1)}, u32[]{:S(2)}) copy-start(bf16[192,192]{1,0:T(8,128)(2,1)} %param.10) | copy-start | bytes 221188
  45.0 19.1 %copy-start.14 = (f32[3,3,3,192]{3,2,1,0:T(4,128)S(1)}, f32[3,3,3,192]{3,2,1,0:T(4,128)}, u32[]{:S(2)}) copy-start(f32[3,3,3,192]{3,2,1,0:T(4,128)} %param.11) | copy-start | bytes 62212
  59.3 7.0 %collective-permute-start = (bf16[16,1,4,192]{3,1,2,0:T(2,128)(2,1)S(1)}, bf16[16,1,4,192]{3,1,2,0:T(2,128)(2,1)S(1)}, u32[]{:S(2)}, u32[]{:S(2)}) collective-permute-start(bf16[16,1,4,192]{3,1,2,0:T(2,128)(2,1)S(1)} %get-tuple-element.97), channel_id=1, source_target_pairs={{0,4},{4,8},{8,12},{12,16},{16,20},{20,24},{24,28},{28,0},{1,5},{5... | collective-permute-start | bytes 73736 | tf_op jit(solution)/shard_map/ppermute | solution.py:25
  60.8 5.6 %collective-permute-start.1 = (bf16[16,1,4,192]{3,1,2,0:T(2,128)(2,1)S(1)}, bf16[16,1,4,192]{3,1,2,0:T(2,128)(2,1)S(1)}, u32[]{:S(2)}, u32[]{:S(2)}) collective-permute-start(bf16[16,1,4,192]{3,1,2,0:T(2,128)(2,1)S(1)} %get-tuple-element.98), channel_id=1, source_target_pairs={{4,0},{8,4},{12,8},{16,12},{20,16},{24,20},{28,24},{0,28},{5,1},{9... | collective-permute-start | bytes 73736 | tf_op jit(solution)/shard_map/ppermute | solution.py:27
  64.7 7.8 %copy-start.17 = (f32[1,1,1,192]{3,2,1,0:T(1,128)}, f32[1,1,1,192]{3,2,1,0:T(1,128)S(1)}, u32[]{:S(2)}) copy-start(f32[1,1,1,192]{3,2,1,0:T(1,128)S(1)} %get-tuple-element.100) | copy-start | bytes 2308
  64.7 7.8 %copy-start.19 = (f32[1,1,1,192]{3,2,1,0:T(1,128)}, f32[1,1,1,192]{3,2,1,0:T(1,128)S(1)}, u32[]{:S(2)}) copy-start(f32[1,1,1,192]{3,2,1,0:T(1,128)S(1)} %get-tuple-element.101) | copy-start | bytes 2308
  64.7 7.8 %copy-start.21 = (f32[1,1,1,192]{3,2,1,0:T(1,128)}, f32[1,1,1,192]{3,2,1,0:T(1,128)S(1)}, u32[]{:S(2)}) copy-start(f32[1,1,1,192]{3,2,1,0:T(1,128)S(1)} %get-tuple-element.102) | copy-start | bytes 2308
  64.7 7.8 %copy-start.23 = (f32[1,1,1,192]{3,2,1,0:T(1,128)}, f32[1,1,1,192]{3,2,1,0:T(1,128)S(1)}, u32[]{:S(2)}) copy-start(f32[1,1,1,192]{3,2,1,0:T(1,128)S(1)} %get-tuple-element.103) | copy-start | bytes 2308
  64.7 7.8 %copy-start.25 = (f32[1,1,1,192]{3,2,1,0:T(1,128)}, f32[1,1,1,192]{3,2,1,0:T(1,128)S(1)}, u32[]{:S(2)}) copy-start(f32[1,1,1,192]{3,2,1,0:T(1,128)S(1)} %get-tuple-element.104) | copy-start | bytes 2308
  64.8 7.8 %copy-start.27 = (f32[1,1,1,192]{3,2,1,0:T(1,128)}, f32[1,1,1,192]{3,2,1,0:T(1,128)S(1)}, u32[]{:S(2)}) copy-start(f32[1,1,1,192]{3,2,1,0:T(1,128)S(1)} %get-tuple-element.105) | copy-start | bytes 2308
  66.5 4.4 %collective-permute-start.2 = (bf16[16,10,1,192]{3,1,2,0:T(8,128)(2,1)S(1)}, bf16[16,10,1,192]{3,1,2,0:T(8,128)(2,1)S(1)}, u32[]{:S(2)}, u32[]{:S(2)}) collective-permute-start(bf16[16,10,1,192]{3,1,2,0:T(8,128)(2,1)S(1)} %get-tuple-element.93), channel_id=1, source_target_pairs={{0,1},{1,2},{2,3},{3,0},{4,5},{5,6},{6,7},{7,4},{8,9},{9,10},{10,1... | collective-permute-start | bytes 184328 | tf_op jit(solution)/shard_map/ppermute | solution.py:25
  66.5 4.8 %collective-permute-start.3 = (bf16[16,10,1,192]{3,1,2,0:T(8,128)(2,1)S(1)}, bf16[16,10,1,192]{3,1,2,0:T(8,128)(2,1)S(1)}, u32[]{:S(2)}, u32[]{:S(2)}) collective-permute-start(bf16[16,10,1,192]{3,1,2,0:T(8,128)(2,1)S(1)} %get-tuple-element.94), channel_id=1, source_target_pairs={{1,0},{2,1},{3,2},{0,3},{5,4},{6,5},{7,6},{4,7},{9,8},{10,9},{11,1... | collective-permute-start | bytes 184328 | tf_op jit(solution)/shard_map/ppermute | solution.py:27
  80.8 7.4 %collective-permute-start.4 = (bf16[16,1,4,192]{3,1,2,0:T(2,128)(2,1)}, bf16[16,1,4,192]{3,1,2,0:T(2,128)(2,1)S(1)}, u32[]{:S(2)}, u32[]{:S(2)}) collective-permute-start(bf16[16,1,4,192]{3,1,2,0:T(2,128)(2,1)} %get-tuple-element.95), channel_id=1, source_target_pairs={{0,4},{4,8},{8,12},{12,16},{16,20},{20,24},{24,28},{28,0},{1,5},{5... | collective-permute-start | bytes 73736 | tf_op jit(solution)/shard_map/ppermute | solution.py:25
  81.5 6.7 %collective-permute-start.5 = (bf16[16,1,4,192]{3,1,2,0:T(2,128)(2,1)}, bf16[16,1,4,192]{3,1,2,0:T(2,128)(2,1)S(1)}, u32[]{:S(2)}, u32[]{:S(2)}) collective-permute-start(bf16[16,1,4,192]{3,1,2,0:T(2,128)(2,1)} %get-tuple-element.96), channel_id=1, source_target_pairs={{4,0},{8,4},{12,8},{16,12},{20,16},{24,20},{28,24},{0,28},{5,1},{9... | collective-permute-start | bytes 73736 | tf_op jit(solution)/shard_map/ppermute | solution.py:27
  88.4 4.4 %collective-permute-start.6 = (bf16[16,10,1,192]{3,1,2,0:T(8,128)(2,1)S(1)}, bf16[16,10,1,192]{3,1,2,0:T(8,128)(2,1)S(1)}, u32[]{:S(2)}, u32[]{:S(2)}) collective-permute-start(bf16[16,10,1,192]{3,1,2,0:T(8,128)(2,1)S(1)} %get-tuple-element.89), channel_id=1, source_target_pairs={{0,1},{1,2},{2,3},{3,0},{4,5},{5,6},{6,7},{7,4},{8,9},{9,10},{10,1... | collective-permute-start | bytes 184328 | tf_op jit(solution)/shard_map/ppermute | solution.py:25
  89.0 4.8 %collective-permute-start.7 = (bf16[16,10,1,192]{3,1,2,0:T(8,128)(2,1)S(1)}, bf16[16,10,1,192]{3,1,2,0:T(8,128)(2,1)S(1)}, u32[]{:S(2)}, u32[]{:S(2)}) collective-permute-start(bf16[16,10,1,192]{3,1,2,0:T(8,128)(2,1)S(1)} %get-tuple-element.90), channel_id=1, source_target_pairs={{1,0},{2,1},{3,2},{0,3},{5,4},{6,5},{7,6},{4,7},{9,8},{10,9},{11,1... | collective-permute-start | bytes 184328 | tf_op jit(solution)/shard_map/ppermute | solution.py:27
  98.4 55.9 %all-to-all-start.2 = ((bf16[16,8,4,192]{3,1,2,0:T(8,128)(2,1)}), bf16[16,8,4,192]{3,1,2,0:T(8,128)(2,1)}, u32[]{:S(2)}, u32[]{:S(2)}) async-start(bf16[16,8,4,192]{3,1,2,0:T(8,128)(2,1)} %convolution_convert_fusion.4), calls=%async_computation.2 | async-start | bytes 524288 | tf_op jit(solution)/shard_map/all_to_all | solution.py:264
  104.2 47.5 %copy-start.6 = (f32[16,8,4,768]{3,1,2,0:T(8,128)S(1)}, f32[16,8,4,768]{3,1,2,0:T(8,128)}, u32[]{:S(2)}) copy-start(f32[16,8,4,768]{3,1,2,0:T(8,128)} %copy-done.5) | copy-start | bytes 4718596
  175.2 20.8 %all-to-all-start.3 = ((bf16[2,64,4,576]{3,2,0,1:T(4,128)(2,1)}), bf16[2,64,4,576]{3,2,0,1:T(4,128)(2,1)S(1)}, u32[]{:S(2)}, u32[]{:S(2)}) async-start(bf16[2,64,4,576]{3,2,0,1:T(4,128)(2,1)} %copy.120), calls=%async_computation.3 | async-start | bytes 1310720 | tf_op jit(solution)/shard_map/all_to_all | solution.py:266
  180.4 151.3 %all-reduce.5.cloned.1.call-start = ((), (), s32[]{:S(2)}) async-start(), calls=%async_computation.4 | async-start | bytes 3735552 | tf_op jit(solution)/shard_map/psum | solution.py:273
  (77 other events, 226.9 us)
Sparse Core Ops, SparseCore 0:
  198.9 132.8 all-reduce.4
where the time goes:
time: 345 us; the launch traced here: 344 us
  waiting for transfers between devices  165 us (48%)
  blocking collectives  54.1 us (16%)
  starting transfers between devices  31.3 us (9%)
  matrix products  29.4 us (9%)
  other arithmetic  24.1 us (7%)
  local copies, waits for them, and re-layouts  24 us (7%)
  between operations  15.6 us (5%)
    psum x1, waiting for transfers between devices, local(): lax.psum((part_qkv, part_out, part_kernel, part_up, part_down), ('gy', 'g...  131 us
    psum x1, blocking collectives, local(): lax.psum((part_qkv, part_out, part_kernel, part_up, part_down), ('gy', 'g...  41.6 us
    all_to_all x1, waiting for transfers between devices, local(): lax.all_to_all(qkv_rows, 'gy', split_axis=0, concat_axis=1, tiled=True)  17 us
    dot_general x6, matrix products, head_product(): jnp.einsum(einsum_form, left_side, right_side, preferred_element_type=jnp...  15.5 us
    all_to_all x1, blocking collectives, attention_exchange_back(): lax.all_to_all(attend(qkv_lines, mask_full, HEADS), 'gy', split_axis=1, c...  12.5 us
    all_to_all x1, waiting for transfers between devices, local(): lax.all_to_all(grad_qkv_lines, 'gy', split_axis=1, concat_axis=0, tiled=T...  12.4 us
    ppermute x4, starting transfers between devices, with_halo(): lax.ppermute(head, axis, [((i + 1) % count, i) for i in range(count)])  10.2 us
    all_to_all x1, starting transfers between devices, local(): lax.all_to_all(qkv_rows, 'gy', split_axis=0, concat_axis=1, tiled=True)  7.25 us
  transfers between devices with their start and end apart: 12, of which 9 were waited for; matrix products, arithmetic and copies ran while one was open for 6% of the time, Pallas kernels for 0%

commit v1 on v0

v1 whole, which is shorter than its diff:
```python
import functools
import math

import jax
import jax.numpy as jnp
from jax import lax
from jax.experimental import pallas as pl
from jax.experimental.pallas import tpu as pltpu
from jax.sharding import PartitionSpec as P

HEADS = 6
BLOCK = 16


NORM_EPS = 1e-05
UNIT_EPS = 1e-06
GELU_SLOPE = 0.7978845608028654
GELU_CUBIC = 0.044715


def norm_rows(values):
    centred = values - jnp.mean(values, axis=-1, keepdims=True)
    inverse = lax.rsqrt(jnp.mean(centred * centred, axis=-1, keepdims=True) + NORM_EPS)
    return (centred * inverse, inverse)


def norm_rows_back(upstream, normal, inverse):
    return inverse * (
        upstream
        - jnp.mean(upstream, axis=-1, keepdims=True)
        - normal * jnp.mean(upstream * normal, axis=-1, keepdims=True)
    )


def unit_scale(values):
    return lax.rsqrt(jnp.mean(values * values, axis=-1, keepdims=True) + UNIT_EPS)


def unit_back(upstream, values, scaling):
    return scaling * upstream - scaling * scaling * scaling * values * jnp.mean(
        upstream * values, axis=-1, keepdims=True
    )


def gelu_value(pre_act):
    return (
        0.5
        * pre_act
        * (1.0 + jnp.tanh(GELU_SLOPE * (pre_act + GELU_CUBIC * pre_act * pre_act * pre_act)))
    )


def gelu_slope(pre_act):
    tangent = jnp.tanh(GELU_SLOPE * (pre_act + GELU_CUBIC * pre_act * pre_act * pre_act))
    return 0.5 * (1.0 + tangent) + 0.5 * pre_act * (1.0 - tangent * tangent) * GELU_SLOPE * (
        1.0 + 3.0 * GELU_CUBIC * pre_act * pre_act
    )


def flatten_rows(values):
    return values.reshape(-1, values.shape[-1])


def project(values, weight):
    summed = jnp.dot(flatten_rows(values), weight, preferred_element_type=jnp.float32)
    return summed.reshape(values.shape[:-1] + (weight.shape[1],))


def project_back(values, weight):
    summed = lax.dot_general(
        flatten_rows(values), weight, (((1,), (1,)), ((), ())), preferred_element_type=jnp.float32
    )
    return summed.reshape(values.shape[:-1] + (weight.shape[0],))


def contract(left_rows, right_rows):
    return lax.dot_general(
        flatten_rows(left_rows),
        flatten_rows(right_rows),
        (((0,), (0,)), ((), ())),
        preferred_element_type=jnp.float32,
    )


def split_heads(values, head_count):
    return values.reshape(values.shape[:-1] + (head_count, values.shape[-1] // head_count))


def join_heads(values):
    return values.reshape(values.shape[:-2] + (values.shape[-2] * values.shape[-1],))


def head_product(einsum_form, left_side, right_side):
    return jnp.einsum(einsum_form, left_side, right_side, preferred_element_type=jnp.float32)


MESH = pl.DeviceIdType.MESH
VMEM = pl.BlockSpec(memory_space=pltpu.VMEM)


def greet(peers):
    barrier = pltpu.get_barrier_semaphore()
    for peer in peers:
        pl.semaphore_signal(barrier, inc=1, device_id=peer, device_id_type=MESH)
    pl.semaphore_wait(barrier, len(peers))


def line_peers(count):
    me_y, me_z = lax.axis_index("gy"), lax.axis_index("gz")
    return [(lax.rem(me_y + k, count), me_z) for k in range(1, count)]


def swap_copies(count, pairs, send_sem, recv_sem):
    me_y, me_z = lax.axis_index("gy"), lax.axis_index("gz")
    copies = []
    for k in range(1, count):
        peer = lax.rem(me_y + k, count)
        for a, (source, target) in enumerate(pairs):
            copies.append(
                pltpu.make_async_remote_copy(
                    src_ref=source.at[peer],
                    dst_ref=target.at[me_y],
                    send_sem=send_sem.at[a, k],
                    recv_sem=recv_sem.at[a, k],
                    device_id=(peer, me_z),
                    device_id_type=MESH,
                )
            )
    return copies


def swap_kernel(count, first_in, second_in, first_out, second_out, send_sem, recv_sem):
    greet(line_peers(count))
    pairs = ((first_in, first_out), (second_in, second_out))
    copies = swap_copies(count, pairs, send_sem, recv_sem)
    for copy in copies:
        copy.start()
    me_y = lax.axis_index("gy")
    for source, target in pairs:
        target[me_y] = source[me_y]
    for copy in copies:
        copy.wait()


def swap_lines(first, second, count):
    shape = jax.ShapeDtypeStruct(first.shape, first.dtype)
    return pl.pallas_call(
        functools.partial(swap_kernel, count),
        out_shape=(shape, shape),
        in_specs=[VMEM, VMEM],
        out_specs=(VMEM, VMEM),
        scratch_shapes=[pltpu.SemaphoreType.DMA((2, count)), pltpu.SemaphoreType.DMA((2, count))],
        compiler_params=pltpu.CompilerParams(collective_id=0, has_side_effects=True),
        name="swap_lines",
    )(first, second)


def face(step, extent):
    return {0: (pl.ds(0, extent), pl.ds(1, extent)), 1: (pl.ds(extent - 1, 1), pl.ds(0, 1)), -1: (pl.ds(0, 1), pl.ds(extent + 1, 1))}[step]


def halo_kernel(count_y, count_z, cells, padded, send_sem, recv_sem):
    me_y, me_z = lax.axis_index("gy"), lax.axis_index("gz")
    extent_x, extent_z = cells.shape[0], cells.shape[1]
    steps = [(dx, dz) for dx in (-1, 0, 1) for dz in (-1, 0, 1) if (dx, dz) != (0, 0)]
    barrier = pltpu.get_barrier_semaphore()

    def reach(dx, action):
        if dx == 0:
            action()
        elif dx == 1:
            pl.when(me_y < count_y - 1)(action)
        else:
            pl.when(me_y > 0)(action)

    def place(dx, dz):
        return (me_y + dx, lax.rem(me_z + dz + count_z, count_z))

    def greet_one(dx, dz):
        pl.semaphore_signal(barrier, inc=1, device_id=place(dx, dz), device_id_type=MESH)

    for dx, dz in steps:
        reach(dx, functools.partial(greet_one, dx, dz))
    inner = (me_y > 0) & (me_y < count_y - 1)

    @pl.when(inner)
    def _():
        pl.semaphore_wait(barrier, 8)

    @pl.when(jnp.logical_not(inner))
    def _():
        pl.semaphore_wait(barrier, 5)

    def copy_of(index):
        dx, dz = steps[index]
        from_x, to_x = face(dx, extent_x)
        from_z, to_z = face(dz, extent_z)
        return pltpu.make_async_remote_copy(
            src_ref=cells.at[from_x, from_z],
            dst_ref=padded.at[to_x, to_z],
            send_sem=send_sem.at[index],
            recv_sem=recv_sem.at[index],
            device_id=place(dx, dz),
            device_id_type=MESH,
        )

    for index, (dx, dz) in enumerate(steps):
        reach(dx, lambda index=index: copy_of(index).start())
    padded[1 : extent_x + 1, 1 : extent_z + 1] = cells[...]
    blank = jnp.zeros((1,) + tuple(padded.shape[1:]), padded.dtype)

    @pl.when(me_y == 0)
    def _():
        padded[0:1] = blank

    @pl.when(me_y == count_y - 1)
    def _():
        padded[extent_x + 1 : extent_x + 2] = blank

    for index, (dx, dz) in enumerate(steps):
        reach(dx, lambda index=index: copy_of(index).wait_send())
        reach(-dx, lambda index=index: copy_of(index).wait_recv())


def halo(cells, count_y, count_z, number):
    shape = (cells.shape[0] + 2, cells.shape[1] + 2) + cells.shape[2:]
    return pl.pallas_call(
        functools.partial(halo_kernel, count_y, count_z),
        out_shape=jax.ShapeDtypeStruct(shape, cells.dtype),
        in_specs=[VMEM],
        out_specs=VMEM,
        scratch_shapes=[pltpu.SemaphoreType.DMA((8,)), pltpu.SemaphoreType.DMA((8,))],
        compiler_params=pltpu.CompilerParams(collective_id=number, has_side_effects=True),
        name="halo%d" % number,
    )(cells)


def bits_of(count_y, count_z):
    levels = []
    for axis, count in (("gz", count_z), ("gy", count_y)):
        bit = 1
        while bit < count:
            levels.append((axis, bit))
            bit *= 2
    return levels


def reduce_kernel(count_y, count_z, parts, first_in, second_in, sums, first_out, second_out, *scratch):
    swap_send, swap_recv, send_sem, recv_sem, total = scratch[:5]
    stages = bits_of(count_y, count_z)
    depth = len(stages)
    outgoing, incoming = scratch[5 : 5 + depth], scratch[5 + depth : 5 + 2 * depth]
    me = {"gy": lax.axis_index("gy"), "gz": lax.axis_index("gz")}
    bit_values, partners = [], []
    for axis, bit in stages:
        value = lax.rem(me[axis] // bit, 2)
        moved = me[axis] + bit * (1 - 2 * value)
        bit_values.append(value)
        partners.append((moved, me["gz"]) if axis == "gy" else (me["gy"], moved))
    greet(line_peers(count_y) + [partner for (axis, _), partner in zip(stages, partners) if axis == "gz"])
    pairs = ((first_in, first_out), (second_in, second_out))
    copies = swap_copies(count_y, pairs, swap_send, swap_recv)
    for copy in copies:
        copy.start()
    for source, target in pairs:
        target[me["gy"]] = source[me["gy"]]
    held, size = parts, parts.shape[0]
    base, bases = 0, []
    for level in range(depth):
        half = size // 2
        keep = base + bit_values[level] * half
        away = base + (1 - bit_values[level]) * half
        outgoing[level][...] = held[pl.ds(away, half)].astype(jnp.bfloat16)
        copy = pltpu.make_async_remote_copy(
            src_ref=outgoing[level],
            dst_ref=incoming[level],
            send_sem=send_sem.at[level],
            recv_sem=recv_sem.at[level],
            device_id=partners[level],
            device_id_type=MESH,
        )
        copy.start()
        copy.wait()
        total[pl.ds(keep, half)] = held[pl.ds(keep, half)] + incoming[level][...].astype(jnp.float32)
        held, base, size = total, keep, half
        bases.append(keep)
    sums[pl.ds(base, size)] = total[pl.ds(base, size)].astype(jnp.bfloat16)
    for level in range(depth - 1, -1, -1):
        span = pl.ds(bases[level], size)
        copy = pltpu.make_async_remote_copy(
            src_ref=sums.at[span],
            dst_ref=sums.at[span],
            send_sem=send_sem.at[depth + level],
            recv_sem=recv_sem.at[depth + level],
            device_id=partners[level],
            device_id_type=MESH,
        )
        copy.start()
        copy.wait()
        size *= 2
    for copy in copies:
        copy.wait()


def reduce_and_swap(parts, first, second, count_y, count_z):
    depth = len(bits_of(count_y, count_z))
    shape = jax.ShapeDtypeStruct(first.shape, first.dtype)
    halves = [
        pltpu.VMEM((parts.shape[0] >> (level + 1),) + parts.shape[1:], jnp.bfloat16)
        for level in range(depth)
    ]
    return pl.pallas_call(
        functools.partial(reduce_kernel, count_y, count_z),
        out_shape=(jax.ShapeDtypeStruct(parts.shape, jnp.bfloat16), shape, shape),
        in_specs=[VMEM, VMEM, VMEM],
        out_specs=(VMEM, VMEM, VMEM),
        scratch_shapes=[
            pltpu.SemaphoreType.DMA((2, count_y)),
            pltpu.SemaphoreType.DMA((2, count_y)),
            pltpu.SemaphoreType.DMA((2 * depth,)),
            pltpu.SemaphoreType.DMA((2 * depth,)),
            pltpu.VMEM(parts.shape, jnp.float32),
        ]
        + halves
        + halves,
        compiler_params=pltpu.CompilerParams(
            collective_id=3, has_side_effects=True, vmem_limit_bytes=24 * 1024 * 1024
        ),
        name="reduce_and_swap",
    )(parts, first, second)


def tiles_of(matrix):
    rows, columns = matrix.shape
    return (
        matrix.reshape(rows // 16, 16, columns // 128, 128)
        .transpose(0, 2, 1, 3)
        .reshape(-1, 16, 128)
    )


def from_tiles(tiles, rows, columns):
    return (
        tiles.reshape(rows // 16, columns // 128, 16, 128)
        .transpose(0, 2, 1, 3)
        .reshape(rows, columns)
    )


def to_lines(swapped, extents):
    planes, part_y, part_z, width = extents
    lines = swapped.reshape(-1, planes, part_y, part_z, width).transpose(1, 3, 0, 2, 4)
    return lines.reshape(planes, part_z, -1, width)


def from_lines(lines, extents):
    planes, part_y, part_z, width = extents
    split = lines.reshape(planes, part_z, -1, part_y, width).transpose(2, 0, 3, 1, 4)
    return split.reshape(split.shape[0], -1, width)

def attention_parts(qkv_rows, mask_full, head_count):
    feature_width = qkv_rows.shape[-1] // 3
    query_vec = qkv_rows[..., :feature_width].astype(jnp.float32)
    key_vec = qkv_rows[..., feature_width : 2 * feature_width].astype(jnp.float32)
    query_scale = unit_scale(query_vec)
    key_scale = unit_scale(key_vec)
    query_unit = (query_vec * query_scale).astype(jnp.bfloat16)
    key_unit = (key_vec * key_scale).astype(jnp.bfloat16)
    factor = 2.0 / math.sqrt(feature_width // head_count)
    scores = head_product(
        "abihd,abjhd->abhij", split_heads(query_unit, head_count), split_heads(key_unit, head_count)
    )
    weights = mask_full * jnp.exp(factor * scores)
    attn_probs = weights / jnp.sum(weights, axis=-1, keepdims=True)
    return (query_vec, key_vec, query_scale, key_scale, query_unit, key_unit, attn_probs, factor)


def attention_forward(token_lines, qkv_weight, out_weight, mask_full):
    token_wide = token_lines.astype(jnp.float32)
    normal, inverse = norm_rows(token_wide)
    normed = normal.astype(jnp.bfloat16)
    qkv_rows = project(normed, qkv_weight).astype(jnp.bfloat16)
    parts = attention_parts(qkv_rows, mask_full, HEADS)
    width = token_lines.shape[-1]
    value_heads = split_heads(qkv_rows[..., 2 * width :], HEADS)
    probs_low = parts[6].astype(jnp.bfloat16)
    attended = join_heads(head_product("abhij,abjhd->abihd", probs_low, value_heads)).astype(
        jnp.bfloat16
    )
    value_field = (token_wide + project(attended, out_weight)).astype(jnp.bfloat16)
    return value_field, (qkv_rows, attended)


def conv_apply(padded, kernel_taps):
    grown = jnp.concatenate([padded[:, :, -1:], padded, padded[:, :, :1]], axis=2)
    extent_x, extent_z, extent_y = padded.shape[0] - 2, padded.shape[1] - 2, padded.shape[2]
    summed = jnp.zeros((extent_x, extent_z, extent_y, padded.shape[3]), jnp.float32)
    for a in range(3):
        for b in range(3):
            for d in range(3):
                window = grown[a : a + extent_x, d : d + extent_z, b : b + extent_y]
                summed = summed + kernel_taps[a, b, d] * window.astype(jnp.float32)
    return summed


def kernel_grad(padded, upstream):
    grown = jnp.concatenate([padded[:, :, -1:], padded, padded[:, :, :1]], axis=2)
    extent_x, extent_z, extent_y, channels = upstream.shape
    upstream_wide = upstream.astype(jnp.float32)
    pieces = []
    for a in range(3):
        for b in range(3):
            for d in range(3):
                window = grown[a : a + extent_x, d : d + extent_z, b : b + extent_y]
                pieces.append(jnp.sum(window.astype(jnp.float32) * upstream_wide, axis=(0, 1, 2)))
    return jnp.stack(pieces)


def feed_forward(padded_value, upstream, conv_kernel, up_weight, down_weight):
    value_field = padded_value[1:-1, 1:-1]
    mixed_field = (value_field.astype(jnp.float32) + conv_apply(padded_value, conv_kernel)).astype(
        jnp.bfloat16
    )
    mixed_wide = mixed_field.astype(jnp.float32)
    normal, inverse = norm_rows(mixed_wide)
    normed = normal.astype(jnp.bfloat16)
    pre_act = project(normed, up_weight)
    hidden = gelu_value(pre_act).astype(jnp.bfloat16)
    block_out = (mixed_wide + project(hidden, down_weight)).astype(jnp.bfloat16)
    grad_hidden = project_back(upstream, down_weight).astype(jnp.bfloat16)
    part_down = contract(upstream, hidden)
    grad_pre = (grad_hidden.astype(jnp.float32) * gelu_slope(pre_act)).astype(jnp.bfloat16)
    part_up = contract(normed, grad_pre)
    grad_normed = project_back(grad_pre, up_weight)
    grad_mixed = (
        upstream.astype(jnp.float32) + norm_rows_back(grad_normed, normal, inverse)
    ).astype(jnp.bfloat16)
    return (block_out, grad_mixed, part_up, part_down)


def attention_backward(
    token_lines, kept, padded_value, padded_grad, conv_kernel, qkv_weight, out_weight, mask_full
):
    qkv_rows, attended = kept
    grad_mixed = padded_grad[1:-1, 1:-1]
    grad_value = (
        grad_mixed.astype(jnp.float32) + conv_apply(padded_grad, conv_kernel[::-1, ::-1, ::-1])
    ).astype(jnp.bfloat16)
    part_kernel = kernel_grad(padded_value, grad_mixed)
    upstream = project_back(grad_value, out_weight).astype(jnp.bfloat16)
    part_out = contract(attended, grad_value)
    query_vec, key_vec, query_scale, key_scale, query_unit, key_unit, attn_probs, factor = (
        attention_parts(qkv_rows, mask_full, HEADS)
    )
    width = token_lines.shape[-1]
    value_heads = split_heads(qkv_rows[..., 2 * width :], HEADS)
    grad_heads = split_heads(upstream, HEADS)
    probs_low = attn_probs.astype(jnp.bfloat16)
    grad_probs = head_product("abihd,abjhd->abhij", grad_heads, value_heads)
    grad_values = head_product("abhij,abihd->abjhd", probs_low, grad_heads)
    grad_scores = attn_probs * (
        grad_probs - jnp.sum(grad_probs * attn_probs, axis=-1, keepdims=True)
    )
    grad_low = (factor * grad_scores).astype(jnp.bfloat16)
    grad_qunit = join_heads(
        head_product("abhij,abjhd->abihd", grad_low, split_heads(key_unit, HEADS))
    )
    grad_kunit = join_heads(
        head_product("abhij,abihd->abjhd", grad_low, split_heads(query_unit, HEADS))
    )
    grad_query = unit_back(grad_qunit, query_vec, query_scale).astype(jnp.bfloat16)
    grad_key = unit_back(grad_kunit, key_vec, key_scale).astype(jnp.bfloat16)
    grad_qkv = jnp.concatenate(
        [grad_query, grad_key, join_heads(grad_values).astype(jnp.bfloat16)], axis=-1
    )
    normal, inverse = norm_rows(token_lines.astype(jnp.float32))
    grad_normed = project_back(grad_qkv, qkv_weight).astype(jnp.bfloat16)
    part_qkv = contract(normal.astype(jnp.bfloat16), grad_qkv)
    token_gradient = (
        grad_value.astype(jnp.float32)
        + norm_rows_back(grad_normed.astype(jnp.float32), normal, inverse)
    ).astype(jnp.bfloat16)
    return token_gradient, jnp.concatenate([part_qkv, part_out], axis=1), part_kernel


def local(tokens, qkv_weight, out_weight, conv_kernel, up_weight, down_weight, band_mask, grad_out):
    count_y, count_z = lax.axis_size("gy"), lax.axis_size("gz")
    extent_x, part_y, part_z, width = tokens.shape
    planes = extent_x // count_y
    extents = (planes, part_y, part_z, width)
    block_count = band_mask.shape[0]
    line_length = block_count * BLOCK
    mask_full = (
        jnp.broadcast_to(band_mask[:, None, :, None], (block_count, BLOCK, block_count, BLOCK))
        .reshape(line_length, line_length)
        .astype(jnp.float32)
    )
    token_swapped, grad_swapped = swap_lines(
        tokens.reshape(count_y, -1, width), grad_out.reshape(count_y, -1, width), count_y
    )
    token_lines = to_lines(token_swapped, extents)
    grad_lines = to_lines(grad_swapped, extents)
    value_field, kept = attention_forward(token_lines, qkv_weight, out_weight, mask_full)
    padded_value = halo(value_field, count_y, count_z, 1)
    block_out, grad_mixed, part_up, part_down = feed_forward(
        padded_value, grad_lines, conv_kernel, up_weight, down_weight
    )
    padded_grad = halo(grad_mixed, count_y, count_z, 2)
    token_gradient, part_qkv_out, part_kernel = attention_backward(
        token_lines, kept, padded_value, padded_grad, conv_kernel, qkv_weight, out_weight, mask_full
    )
    hidden_width = up_weight.shape[1]
    pieces = [tiles_of(part_up), tiles_of(part_down), tiles_of(part_qkv_out)]
    kernel_flat = part_kernel.reshape(-1)
    kernel_tiles = -(-kernel_flat.shape[0] // 2048)
    used = sum(piece.shape[0] for piece in pieces)
    devices = count_y * count_z
    whole = -(-(used + kernel_tiles) // devices) * devices
    tail = jnp.pad(kernel_flat, (0, (whole - used) * 2048 - kernel_flat.shape[0]))
    parts = jnp.concatenate(pieces + [tail.reshape(-1, 16, 128)], axis=0)
    sums, block_swapped, token_swapped = reduce_and_swap(
        parts, from_lines(block_out, extents), from_lines(token_gradient, extents), count_y, count_z
    )
    factor = 1.0 / math.sqrt(extent_x * part_y * count_y * part_z * count_z)
    scaled = sums.astype(jnp.float32) * factor
    one = pieces[0].shape[0]
    up_sum = from_tiles(scaled[:one], width, hidden_width)
    down_sum = from_tiles(scaled[one : 2 * one], width, hidden_width).T
    joint = from_tiles(scaled[2 * one : used], width, 4 * width)
    kernel_sum = scaled[used:].reshape(-1)[: kernel_flat.shape[0]].reshape(conv_kernel.shape)
    return (
        block_swapped.reshape(tokens.shape),
        token_swapped.reshape(tokens.shape),
        joint[:, : 3 * width],
        joint[:, 3 * width :],
        kernel_sum,
        up_sum,
        down_sum,
    )


def solution(mesh):
    placed = (P(None, "gy", "gz", None), P(), P(), P(), P(), P(), P(), P(None, "gy", "gz", None))
    return jax.shard_map(
        local,
        mesh=mesh,
        in_specs=placed,
        out_specs=(P(None, "gy", "gz", None), P(None, "gy", "gz", None), P(), P(), P(), P(), P()),
        check_vma=False,
    )
```

time: 345 us -> 178 us (0.52)
  waiting for transfers between devices: 165 us -> 0 us
  Pallas kernels: 0 us -> 88.1 us
  blocking collectives: 54.1 us -> 0 us
  starting transfers between devices: 31.3 us -> 0 us
  between operations: 15.6 us -> 2.29 us
  local copies, waits for them, and re-layouts: 24 us -> 30.5 us
  other arithmetic: 24.1 us -> 28.7 us
    psum x1 -> x0, waiting for transfers between devices: 131 us -> none  [local(): lax.psum((part_qkv, part_out, part_kernel, part_up, part_down), ('gy', 'g...]
    pallas_call x0 -> x4, Pallas kernels: none -> 88.1 us  [the longest x1 43.7 us: reduce_and_swap(): pl.pallas_call(functools.partial(reduce_kernel, count_y, count_z), out_sh...]
    psum x1 -> x0, blocking collectives: 41.6 us -> none  [local(): lax.psum((part_qkv, part_out, part_kernel, part_up, part_down), ('gy', 'g...]
    all_to_all x3 -> x0, waiting for transfers between devices: 29.3 us -> none  [the longest x1 17 us: local(): lax.all_to_all(qkv_rows, 'gy', split_axis=0, concat_axis=1, tiled=True)]
    all_to_all x3 -> x0, starting transfers between devices: 18.2 us -> none  [the longest x1 7.25 us: local(): lax.all_to_all(qkv_rows, 'gy', split_axis=0, concat_axis=1, tiled=True)]
    ppermute x8 -> x0, starting transfers between devices: 13.1 us -> none  [the longest x4 10.2 us: with_halo(): lax.ppermute(head, axis, [((i + 1) % count, i) for i in range(count)])]
    all_to_all x1 -> x0, blocking collectives: 12.5 us -> none  [attention_exchange_back(): lax.all_to_all(attend(qkv_lines, mask_full, HEADS), 'gy', split_axis=1, c...]
    mul x5 -> x1, other arithmetic: 5.89 us -> 0.12 us  [local(): scaled = sums.astype(jnp.float32) * factor]
  transfers between devices with their start and end apart: 12 -> 0, of which waited for: 9 -> 0; matrix products, arithmetic and copies ran while one was open for 6% -> 0% of each run, Pallas kernels for 0% -> 0%
where the time goes in v1:
time: 178 us
  Pallas kernels  88.1 us (49%)
  local copies, waits for them, and re-layouts  30.5 us (17%)
  other arithmetic  28.7 us (16%)
  matrix products  28.1 us (16%)
  between operations  2.29 us (1%)
    pallas_call x1, Pallas kernels, reduce_and_swap(): pl.pallas_call(functools.partial(reduce_kernel, count_y, count_z), out_sh...  43.7 us
    pallas_call x2, Pallas kernels, halo(): pl.pallas_call(functools.partial(halo_kernel, count_y, count_z), out_shap...  27.9 us
    pallas_call x1, Pallas kernels, swap_lines(): pl.pallas_call(functools.partial(swap_kernel, count), out_shape=(shape, s...  16.5 us
    dot_general x6, matrix products, head_product(): jnp.einsum(einsum_form, left_side, right_side, preferred_element_type=jnp...  16.5 us
    reduce_sum x2, other arithmetic, norm_rows(): centred = values - jnp.mean(values, axis=-1, keepdims=True)  7.25 us
    unnamed x199, local copies, waits for them, and re-layouts  6.24 us
    dot_general x4, matrix products, project_back(): lax.dot_general(flatten_rows(values), weight, (((1,), (1,)), ((), ())), p...  5.21 us
    reduce_sum x4, other arithmetic, kernel_grad(): jnp.sum(window.astype(jnp.float32) * upstream_wide, axis=(0, 1, 2))  4.77 us

profile of v1, /device:TPU:0, one launch (start us, length us, event | category | flops | bytes accessed | tf_op | source)
XLA Modules:
  0.0 177.7 jit_solution(12987124118409796964)
XLA Ops:
  0.6 1.9 %reshape.288.first_in = bf16[8,64,192]{2,1,0:T(8,128)(2,1)} reshape(bf16[16,8,4,192]{3,2,1,0:T(4,128)(2,1)} %param.8) | data formatting | bytes 393216 | tf_op jit(solution)/shard_map/reshape | solution.py:499
  2.5 1.9 %reshape.289.second_in = bf16[8,64,192]{2,1,0:T(8,128)(2,1)} reshape(bf16[16,8,4,192]{3,2,1,0:T(4,128)(2,1)} %param.15) | data formatting | bytes 393216 | tf_op jit(solution)/shard_map/reshape | solution.py:499
  4.4 16.5 %swap_lines.1 = (bf16[8,64,192]{2,1,0:T(8,128)(2,1)}, bf16[8,64,192]{2,1,0:T(8,128)(2,1)}) custom-call(bf16[8,64,192]{2,1,0:T(8,128)(2,1)} %reshape.288.first_in, bf16[8,64,192]{2,1,0:T(8,128)(2,1)} %reshape.289.second_in), custom_call_target="tpu_custom_call" | custom-call | tf_op jit(solution)/shard_map/swap_lines/pallas_call | solution.py:147
  25.6 1.6 exponential_multiply_fusion
  27.3 2.3 %convolution_convert_fusion.3 = bf16[2,4,6,32,64]{4,3,2,1,0:T(8,128)(2,1)S(1)} fusion(bf16[2,4,64,6,32]{2,4,3,1,0:T(8,128)(2,1)S(1)} %bitcast.257, f32[2,4,6,64,64]{3,4,2,1,0:T(8,128)} %exponential_multiply_fusion), kind=kOutput, calls=%fused_computation.83 | convolution fusion | flops 13077567 | bytes 1179648 | tf_op jit(solution)/shard_map/abhij,abjhd->abihd/dot_general | solution.py:94
  30.6 14.4 %halo1.1 = bf16[4,6,64,192]{3,2,1,0:T(8,128)(2,1)} custom-call(bf16[2,4,64,192]{3,2,1,0:T(8,128)(2,1)} %fusion.18.cells), custom_call_target="tpu_custom_call" | custom-call | tf_op jit(solution)/shard_map/halo1/pallas_call | solution.py:227
  46.3 7.1 %convert_reduce_fusion = (f32[2,4,64]{2,1,0:T(4,128)S(1)}, bf16[2,4,64,192]{3,2,1,0:T(8,128)(2,1)S(1)}, bf16[2,4,64,192]{3,2,1,0:T(8,128)(2,1)}, bf16[2,4,64,192]{3,2,1,0:T(8,128)(2,1)}) fusion(f32[192]{0:T(256)S(1)} %bitcast.299, f32[192]{0:T(256)S(1)} %bitcast.302, f32[192]{0:T(256)S(1)} %bitcast.308, bf16[4,6,64,192]{3,2,1,0:T(8,128)(2,1)} %halo1.1, ...), kind=kLoop, calls=%fused_computation.103 | loop fusion | flops 13762048 | bytes 3776768 | tf_op jit(solution)/shard_map/reduce_sum | solution.py:22
  54.0 2.0 %multiply_convert_fusion.1 = (bf16[2,4,64,768]{3,2,1,0:T(8,128)(2,1)}, f32[2,4,64,768]{3,2,1,0:T(8,128)}) fusion(bf16[2,4,64,192]{3,2,1,0:T(8,128)(2,1)S(1)} %fusion.29, bf16[192,768]{1,0:T(8,128)(2,1)S(1)} %copy-done), kind=kOutput, calls=%fused_computation.76 | convolution fusion | flops 154533888 | bytes 2850816 | tf_op jit(solution)/shard_map/dot_general | solution.py:65
  56.1 2.6 %fusion.7 = bf16[2,4,64,768]{3,2,1,0:T(8,128)(2,1)S(1)} fusion(f32[2,4,64,768]{3,2,1,0:T(8,128)} %get-tuple-element.111, bf16[768,192]{0,1:T(8,128)(2,1)S(1)} %copy-done.26, bf16[8,2,8,4,192]{4,3,2,1,0:T(4,128)(2,1)S(1)} %reshape.294), kind=kOutput, calls=%fused_computation.72 | convolution fusion | flops 159252480 | bytes 2850816 | tf_op jit(solution)/shard_map/dot_general | solution.py:70
  61.1 13.4 %halo2.1 = bf16[4,6,64,192]{3,2,1,0:T(8,128)(2,1)} custom-call(bf16[2,4,64,192]{3,2,1,0:T(8,128)(2,1)} %fusion.34.cells), custom_call_target="tpu_custom_call" | custom-call | tf_op jit(solution)/shard_map/halo2/pallas_call | solution.py:227
  74.6 1.5 fusion.107
  76.1 1.6 fusion.114
  79.3 2.1 %stack.111 = f32[27,192]{1,0:T(8,128)S(1)} concatenate(f32[1,192]{1,0:T(1,128)S(1)} %bitcast.378, f32[1,192]{1,0:T(1,128)S(1)} %bitcast.379, f32[1,192]{1,0:T(1,128)S(1)} %bitcast.380, f32[1,192]{1,0:T(1,128)S(1)} %bitcast.365, f32[1,192]{1,0:T(1,128)S(1)} %bitcast.366, f32[1,192]{1,0:T(1,128)S(1)} %bitcast.367, f32[1,192]{1,0:T(1,128)} %bitcast.385, f32[1,192]{1,0:T(1,128)} %bitcast.386, ...), dimensions={0} | concatenate | bytes 41472 | tf_op jit(solution)/shard_map/stack | solution.py:416
  82.5 3.0 %fusion.119 = bf16[2,4,64,192]{3,2,1,0:T(8,128)(2,1)S(1)} fusion(bf16[4,6,64,192]{3,2,1,0:T(8,128)(2,1)S(1)} %copy-done.4, bf16[4,6,1,192]{3,2,1,0:T(2,128)(2,1)S(1)} %get-tuple-element.71, bf16[4,6,1,192]{3,2,1,0:T(2,128)(2,1)S(1)} %get-tuple-element.70, f32[192]{0:T(256)S(1)} %bitcast.300, f32[192]{0:T(256)S(1)} %bitcast.303, f32[192]{0:T(256)S(1)} %bitcast.309, ...), kind=kLoop, calls=%fused_computation.240 | loop fusion | flops 13369344 | bytes 3419136 | tf_op jit(solution)/shard_map/convert_element_type | solution.py:448
  86.3 2.4 %convolution_convert_fusion.2 = bf16[2,4,6,32,64]{4,3,2,1,0:T(8,128)(2,1)S(1)} fusion(bf16[2,4,64,6,32]{2,4,3,1,0:T(8,128)(2,1)S(1)} %bitcast.263, f32[2,4,6,64,64]{3,4,2,1,0:T(8,128)} %exponential_multiply_fusion), kind=kOutput, calls=%fused_computation.82 | convolution fusion | flops 13077567 | bytes 1179648 | tf_op jit(solution)/shard_map/abhij,abihd->abjhd/dot_general | solution.py:94
  89.7 3.2 %fusion.22 = f32[2,4,6,64,64]{3,4,2,1,0:T(8,128)} fusion(f32[2,4,6,64,64]{3,4,2,1,0:T(8,128)} %exponential_multiply_fusion), kind=kOutput, calls=%fused_computation.107 | output fusion | flops 199743 | bytes 1572864 | tf_op jit(solution)/shard_map/div | solution.py:374
  92.9 1.6 fusion.188
  94.5 4.2 %fusion.15 = f32[2,4,6,32,64]{4,3,2,1,0:T(8,128)} fusion(bf16[2,4,64,6,32]{2,4,3,1,0:T(8,128)(2,1)S(1)} %bitcast.262, f32[2,4,6,64,64]{3,4,2,1,0:T(8,128)} %fusion.22, f32[2,4,6,64,64]{3,4,2,1,0:T(8,128)} %fusion.188), kind=kOutput, calls=%fused_computation.79 | convolution fusion | flops 13569087 | bytes 2162688 | tf_op jit(solution)/shard_map/abhij,abjhd->abihd/dot_general | solution.py:94
  98.7 1.4 copy.59
  100.2 4.4 %fusion.12 = f32[2,4,6,32,64]{4,3,2,1,0:T(8,128)} fusion(bf16[2,4,64,6,32]{2,4,3,1,0:T(8,128)(2,1)} %bitcast.260, f32[2,4,6,64,64]{3,4,2,1,0:T(8,128)} %fusion.22, f32[2,4,6,64,64]{3,4,2,1,0:T(8,128)} %fusion.188), kind=kOutput, calls=%fused_computation.78 | convolution fusion | flops 13569087 | bytes 2162688 | tf_op jit(solution)/shard_map/abhij,abihd->abjhd/dot_general | solution.py:94
  104.5 2.2 %copy.62 = f32[2,4,64,192]{3,2,1,0:T(8,128)} copy(f32[2,4,64,192]{2,3,1,0:T(8,128)} %bitcast.274) | data formatting | bytes 786432 | tf_op jit(solution)/shard_map/reshape | solution.py:90
  120.3 1.9 %fusion.178 = (f32[2,4,64]{2,1,0:T(4,128)S(1)}, f32[2,4,64]{2,1,0:T(4,128)S(1)}, f32[2,4,64,192]{3,2,1,0:T(8,128)S(1)}) fusion(f32[2,4,64]{2,1,0:T(4,128)S(1)} %copy-done.36, f32[2,4,64]{2,1,0:T(4,128)S(1)} %copy-done.39, f32[8,2,8,4,192]{4,3,2,1,0:T(4,128)} %copy-done.5, bf16[192,576]{1,0:T(8,128)(2,1)} %param.9, bf16[2,4,64,192]{3,2,1,0:T(8,128)(2,1)} %copy.65, ...), kind=kOutput, calls=%fused_computation.349 | convolution fusion | flops 115702784 | bytes 1605632 | tf_op jit(solution)/shard_map/dot_general | solution.py:70
  122.5 3.4 %fusion.161 = bf16[2,4,8,8,192]{4,3,2,1,0:T(8,128)(2,1)S(1)} fusion(f32[8,2,8,4,192]{4,3,2,1,0:T(4,128)S(1)} %copy-done.6, f32[2,4,64,192]{3,2,1,0:T(8,128)S(1)} %get-tuple-element.112, f32[2,4,64]{2,1,0:T(4,128)S(1)} %broadcast_multiply_fusion.1, f32[2,4,64]{2,1,0:T(4,128)S(1)} %broadcast_multiply_fusion.2, f32[2,4,64]{2,1,0:T(4,128)S(1)} %copy-done.36, ...), kind=kLoop, calls=%fused_computation.314 | loop fusion | flops 14254080 | bytes 4484096 | tf_op jit(solution)/shard_map/reshape | solution.py:358
  126.3 43.7 %reduce_and_swap.1 = (bf16[224,16,128]{2,1,0:T(8,128)(2,1)S(1)}, bf16[8,64,192]{2,1,0:T(8,128)(2,1)S(1)}, bf16[8,64,192]{2,1,0:T(8,128)(2,1)S(1)}) custom-call(f32[224,16,128]{2,1,0:T(8,128)S(1)} %pad_maximum_fusion.parts, bf16[8,64,192]{2,1,0:T(8,128)(2,1)S(1)} %reshape.307.first_in, bf16[8,64,192]{2,1,0:T(8,128)(2,1)S(1)} %reshape.309.second_in), custom_call_target="tpu_custom_call" | custom-call | tf_op jit(solution)/shard_map/reduce_and_swap/pallas_call | solution.py:312
  (275 shorter events, 35.0 us)
Async XLA Ops:
  0.6 53.3 %copy-start = (bf16[192,768]{1,0:T(8,128)(2,1)S(1)}, bf16[192,768]{1,0:T(8,128)(2,1)}, u32[]{:S(2)}) copy-start(bf16[192,768]{1,0:T(8,128)(2,1)} %param.12) | copy-start | bytes 884740
  22.0 87.6 %copy-start.5 = (f32[8,2,8,4,192]{4,3,2,1,0:T(4,128)}, f32[8,2,8,4,192]{4,3,2,1,0:T(4,128)S(1)}, u32[]{:S(2)}) copy-start(f32[8,2,8,4,192]{4,3,2,1,0:T(4,128)S(1)} %reshape.322) | copy-start | bytes 1179652
  46.0 36.2 %copy-start.43 = (f32[1,1,1,192]{3,2,1,0:T(1,128)}, f32[1,1,1,192]{3,2,1,0:T(1,128)S(1)}, u32[]{:S(2)}) copy-start(f32[1,1,1,192]{3,2,1,0:T(1,128)S(1)} %get-tuple-element.97) | copy-start | bytes 2308
  46.0 36.2 %copy-start.45 = (f32[1,1,1,192]{3,2,1,0:T(1,128)}, f32[1,1,1,192]{3,2,1,0:T(1,128)S(1)}, u32[]{:S(2)}) copy-start(f32[1,1,1,192]{3,2,1,0:T(1,128)S(1)} %get-tuple-element.98) | copy-start | bytes 2308
  46.0 36.2 %copy-start.47 = (f32[1,1,1,192]{3,2,1,0:T(1,128)}, f32[1,1,1,192]{3,2,1,0:T(1,128)S(1)}, u32[]{:S(2)}) copy-start(f32[1,1,1,192]{3,2,1,0:T(1,128)S(1)} %get-tuple-element.99) | copy-start | bytes 2308
  46.0 36.2 %copy-start.49 = (f32[1,1,1,192]{3,2,1,0:T(1,128)}, f32[1,1,1,192]{3,2,1,0:T(1,128)S(1)}, u32[]{:S(2)}) copy-start(f32[1,1,1,192]{3,2,1,0:T(1,128)S(1)} %get-tuple-element.100) | copy-start | bytes 2308
  46.1 36.2 %copy-start.51 = (f32[1,1,1,192]{3,2,1,0:T(1,128)}, f32[1,1,1,192]{3,2,1,0:T(1,128)S(1)}, u32[]{:S(2)}) copy-start(f32[1,1,1,192]{3,2,1,0:T(1,128)S(1)} %get-tuple-element.101) | copy-start | bytes 2308
  46.1 36.2 %copy-start.53 = (f32[1,1,1,192]{3,2,1,0:T(1,128)}, f32[1,1,1,192]{3,2,1,0:T(1,128)S(1)}, u32[]{:S(2)}) copy-start(f32[1,1,1,192]{3,2,1,0:T(1,128)S(1)} %get-tuple-element.102) | copy-start | bytes 2308
  46.1 36.2 %copy-start.55 = (f32[1,1,1,192]{3,2,1,0:T(1,128)}, f32[1,1,1,192]{3,2,1,0:T(1,128)S(1)}, u32[]{:S(2)}) copy-start(f32[1,1,1,192]{3,2,1,0:T(1,128)S(1)} %get-tuple-element.103) | copy-start | bytes 2308
  46.1 36.2 %copy-start.57 = (f32[1,1,1,192]{3,2,1,0:T(1,128)}, f32[1,1,1,192]{3,2,1,0:T(1,128)S(1)}, u32[]{:S(2)}) copy-start(f32[1,1,1,192]{3,2,1,0:T(1,128)S(1)} %get-tuple-element.104) | copy-start | bytes 2308
  46.1 36.2 %copy-start.59 = (f32[1,1,1,192]{3,2,1,0:T(1,128)}, f32[1,1,1,192]{3,2,1,0:T(1,128)S(1)}, u32[]{:S(2)}) copy-start(f32[1,1,1,192]{3,2,1,0:T(1,128)S(1)} %get-tuple-element.78) | copy-start | bytes 2308
  46.1 36.2 %copy-start.61 = (f32[1,1,1,192]{3,2,1,0:T(1,128)}, f32[1,1,1,192]{3,2,1,0:T(1,128)S(1)}, u32[]{:S(2)}) copy-start(f32[1,1,1,192]{3,2,1,0:T(1,128)S(1)} %get-tuple-element.79) | copy-start | bytes 2308
  46.1 36.2 %copy-start.63 = (f32[1,1,1,192]{3,2,1,0:T(1,128)}, f32[1,1,1,192]{3,2,1,0:T(1,128)S(1)}, u32[]{:S(2)}) copy-start(f32[1,1,1,192]{3,2,1,0:T(1,128)S(1)} %get-tuple-element.80) | copy-start | bytes 2308
  46.2 36.2 %copy-start.65 = (f32[1,1,1,192]{3,2,1,0:T(1,128)}, f32[1,1,1,192]{3,2,1,0:T(1,128)S(1)}, u32[]{:S(2)}) copy-start(f32[1,1,1,192]{3,2,1,0:T(1,128)S(1)} %get-tuple-element.81) | copy-start | bytes 2308
  46.2 36.2 %copy-start.67 = (f32[1,1,1,192]{3,2,1,0:T(1,128)}, f32[1,1,1,192]{3,2,1,0:T(1,128)S(1)}, u32[]{:S(2)}) copy-start(f32[1,1,1,192]{3,2,1,0:T(1,128)S(1)} %get-tuple-element.82) | copy-start | bytes 2308
  46.2 36.2 %copy-start.69 = (f32[1,1,1,192]{3,2,1,0:T(1,128)}, f32[1,1,1,192]{3,2,1,0:T(1,128)S(1)}, u32[]{:S(2)}) copy-start(f32[1,1,1,192]{3,2,1,0:T(1,128)S(1)} %get-tuple-element.83) | copy-start | bytes 2308
  46.2 36.2 %copy-start.71 = (f32[1,1,1,192]{3,2,1,0:T(1,128)}, f32[1,1,1,192]{3,2,1,0:T(1,128)S(1)}, u32[]{:S(2)}) copy-start(f32[1,1,1,192]{3,2,1,0:T(1,128)S(1)} %get-tuple-element.84) | copy-start | bytes 2308
  46.2 36.2 %copy-start.73 = (f32[1,1,1,192]{3,2,1,0:T(1,128)}, f32[1,1,1,192]{3,2,1,0:T(1,128)S(1)}, u32[]{:S(2)}) copy-start(f32[1,1,1,192]{3,2,1,0:T(1,128)S(1)} %get-tuple-element.85) | copy-start | bytes 2308
  46.2 36.2 %copy-start.75 = (f32[1,1,1,192]{3,2,1,0:T(1,128)}, f32[1,1,1,192]{3,2,1,0:T(1,128)S(1)}, u32[]{:S(2)}) copy-start(f32[1,1,1,192]{3,2,1,0:T(1,128)S(1)} %get-tuple-element.86) | copy-start | bytes 2308
  46.2 36.2 %copy-start.77 = (f32[1,1,1,192]{3,2,1,0:T(1,128)}, f32[1,1,1,192]{3,2,1,0:T(1,128)S(1)}, u32[]{:S(2)}) copy-start(f32[1,1,1,192]{3,2,1,0:T(1,128)S(1)} %get-tuple-element.87) | copy-start | bytes 2308
  46.2 36.2 %copy-start.79 = (f32[1,1,1,192]{3,2,1,0:T(1,128)}, f32[1,1,1,192]{3,2,1,0:T(1,128)S(1)}, u32[]{:S(2)}) copy-start(f32[1,1,1,192]{3,2,1,0:T(1,128)S(1)} %get-tuple-element.88) | copy-start | bytes 2308
  46.2 36.2 %copy-start.81 = (f32[1,1,1,192]{3,2,1,0:T(1,128)}, f32[1,1,1,192]{3,2,1,0:T(1,128)S(1)}, u32[]{:S(2)}) copy-start(f32[1,1,1,192]{3,2,1,0:T(1,128)S(1)} %get-tuple-element.89) | copy-start | bytes 2308
  46.2 36.2 %copy-start.83 = (f32[1,1,1,192]{3,2,1,0:T(1,128)}, f32[1,1,1,192]{3,2,1,0:T(1,128)S(1)}, u32[]{:S(2)}) copy-start(f32[1,1,1,192]{3,2,1,0:T(1,128)S(1)} %get-tuple-element.90) | copy-start | bytes 2308
  46.3 36.2 %copy-start.85 = (f32[1,1,1,192]{3,2,1,0:T(1,128)}, f32[1,1,1,192]{3,2,1,0:T(1,128)S(1)}, u32[]{:S(2)}) copy-start(f32[1,1,1,192]{3,2,1,0:T(1,128)S(1)} %get-tuple-element.91) | copy-start | bytes 2308
  (74 other events, 388.0 us)

commit v2 on v1

--- a/solution.py
+++ b/solution.py
@@ -40,58 +40,6 @@
     return scaling * upstream - scaling * scaling * scaling * values * jnp.mean(
         upstream * values, axis=-1, keepdims=True
     )
-
-
-def gelu_value(pre_act):
-    return (
-        0.5
-        * pre_act
-        * (1.0 + jnp.tanh(GELU_SLOPE * (pre_act + GELU_CUBIC * pre_act * pre_act * pre_act)))
-    )
-
-
-def gelu_slope(pre_act):
-    tangent = jnp.tanh(GELU_SLOPE * (pre_act + GELU_CUBIC * pre_act * pre_act * pre_act))
-    return 0.5 * (1.0 + tangent) + 0.5 * pre_act * (1.0 - tangent * tangent) * GELU_SLOPE * (
-        1.0 + 3.0 * GELU_CUBIC * pre_act * pre_act
-    )
-
-
-def flatten_rows(values):
-    return values.reshape(-1, values.shape[-1])
-
-
-def project(values, weight):
-    summed = jnp.dot(flatten_rows(values), weight, preferred_element_type=jnp.float32)
-    return summed.reshape(values.shape[:-1] + (weight.shape[1],))
-
-
-def project_back(values, weight):
-    summed = lax.dot_general(
-        flatten_rows(values), weight, (((1,), (1,)), ((), ())), preferred_element_type=jnp.float32
-    )
-    return summed.reshape(values.shape[:-1] + (weight.shape[0],))
-
-
-def contract(left_rows, right_rows):
-    return lax.dot_general(
-        flatten_rows(left_rows),
-        flatten_rows(right_rows),
-        (((0,), (0,)), ((), ())),
-        preferred_element_type=jnp.float32,
-    )
-
-
-def split_heads(values, head_count):
-    return values.reshape(values.shape[:-1] + (head_count, values.shape[-1] // head_count))
-
-
-def join_heads(values):
-    return values.reshape(values.shape[:-2] + (values.shape[-2] * values.shape[-1],))
-
-
-def head_product(einsum_form, left_side, right_side):
-    return jnp.einsum(einsum_form, left_side, right_side, preferred_element_type=jnp.float32)
 
 
 MESH = pl.DeviceIdType.MESH
@@ -330,19 +278,10 @@
     )(parts, first, second)
 
 
-def tiles_of(matrix):
-    rows, columns = matrix.shape
-    return (
-        matrix.reshape(rows // 16, 16, columns // 128, 128)
-        .transpose(0, 2, 1, 3)
-        .reshape(-1, 16, 128)
-    )
-
-
 def from_tiles(tiles, rows, columns):
     return (
-        tiles.reshape(rows // 16, columns // 128, 16, 128)
-        .transpose(0, 2, 1, 3)
+        tiles.reshape(columns // 128, rows, 128)
+        .transpose(1, 0, 2)
         .reshape(rows, columns)
     )
 
@@ -358,129 +297,261 @@
     split = lines.reshape(planes, part_z, -1, part_y, width).transpose(2, 0, 3, 1, 4)
     return split.reshape(split.shape[0], -1, width)
 
-def attention_parts(qkv_rows, mask_full, head_count):
-    feature_width = qkv_rows.shape[-1] // 3
-    query_vec = qkv_rows[..., :feature_width].astype(jnp.float32)
-    key_vec = qkv_rows[..., feature_width : 2 * feature_width].astype(jnp.float32)
-    query_scale = unit_scale(query_vec)
-    key_scale = unit_scale(key_vec)
-    query_unit = (query_vec * query_scale).astype(jnp.bfloat16)
+def dot(left, right, left_axis=1, right_axis=0):
+    return lax.dot_general(
+        left, right, (((left_axis,), (right_axis,)), ((), ())), preferred_element_type=jnp.float32
+    )
+
+
+def stack_heads(values):
+    width = values.shape[1]
+    head_of = lax.broadcasted_iota(jnp.int32, (1, width), 1) // (width // HEADS)
+    return jnp.concatenate([jnp.where(head_of == h, values, 0.0) for h in range(HEADS)], axis=0)
+
+
+def unstack_heads(stacked):
+    rows, width = stacked.shape[0] // HEADS, stacked.shape[1]
+    head_of = lax.broadcasted_iota(jnp.int32, (1, width), 1) // (width // HEADS)
+    joined = stacked[:rows]
+    for h in range(1, HEADS):
+        joined = jnp.where(head_of == h, stacked[h * rows : (h + 1) * rows], joined)
+    return joined
+
+
+def line_probs(query_vec, key_vec, mask_stack):
+    query_scale, key_scale = unit_scale(query_vec), unit_scale(key_vec)
+    query_stack = stack_heads(query_vec * query_scale).astype(jnp.bfloat16)
     key_unit = (key_vec * key_scale).astype(jnp.bfloat16)
-    factor = 2.0 / math.sqrt(feature_width // head_count)
-    scores = head_product(
-        "abihd,abjhd->abhij", split_heads(query_unit, head_count), split_heads(key_unit, head_count)
-    )
-    weights = mask_full * jnp.exp(factor * scores)
-    attn_probs = weights / jnp.sum(weights, axis=-1, keepdims=True)
-    return (query_vec, key_vec, query_scale, key_scale, query_unit, key_unit, attn_probs, factor)
+    factor = 2.0 / math.sqrt(query_vec.shape[1] // HEADS)
+    weights = mask_stack * jnp.exp(factor * dot(query_stack, key_unit, 1, 1))
+    probs = weights / jnp.sum(weights, axis=-1, keepdims=True)
+    return query_scale, key_scale, query_stack, key_unit, probs, factor
+
+
+def forward_kernel(tokens, qkv_weight, out_weight, mask, field, query, key, value, attended):
+    planes, part_z, length, width = tokens.shape
+    lines = planes * part_z
+    token_wide = tokens[...].reshape(lines * length, width).astype(jnp.float32)
+    normal, _ = norm_rows(token_wide)
+    normed = normal.astype(jnp.bfloat16)
+    for piece, target in enumerate((query, key, value)):
+        weight = qkv_weight[:, piece * width : (piece + 1) * width]
+        target[...] = dot(normed, weight).astype(jnp.bfloat16)
+    for line in range(lines):
+        rows = pl.ds(line * length, length)
+        probs = line_probs(
+            query[rows].astype(jnp.float32), key[rows].astype(jnp.float32), mask[...]
+        )[4]
+        attended[rows] = unstack_heads(dot(probs.astype(jnp.bfloat16), value[rows])).astype(
+            jnp.bfloat16
+        )
+    field[...] = (
+        (token_wide + dot(attended[...], out_weight[...])).astype(jnp.bfloat16).reshape(field.shape)
+    )
+
+
+def single(body, name, outs, scratch, *operands):
+    return pl.pallas_call(
+        body,
+        out_shape=outs,
+        in_specs=[VMEM] * len(operands),
+        out_specs=[VMEM] * len(outs),
+        scratch_shapes=scratch,
+        compiler_params=pltpu.CompilerParams(vmem_limit_bytes=32 * 1024 * 1024),
+        name=name,
+    )(*operands)
+
+
+def low(*shape):
+    return jax.ShapeDtypeStruct(shape, jnp.bfloat16)
+
+
+def wide(*shape):
+    return jax.ShapeDtypeStruct(shape, jnp.float32)
+
+
+def stacked_mask(mask_full):
+    return jnp.tile(mask_full, (HEADS, 1))
 
 
 def attention_forward(token_lines, qkv_weight, out_weight, mask_full):
-    token_wide = token_lines.astype(jnp.float32)
-    normal, inverse = norm_rows(token_wide)
+    width = token_lines.shape[-1]
+    count = token_lines.size // width
+    flat = low(count, width)
+    field, *kept = single(
+        forward_kernel,
+        "attention_forward",
+        (low(*token_lines.shape), flat, flat, flat, flat),
+        [],
+        token_lines,
+        qkv_weight,
+        out_weight,
+        stacked_mask(mask_full),
+    )
+    return field, kept
+
+
+def shift_rows(values, step):
+    return pltpu.roll(values, step % values.shape[0], 0)
+
+
+def conv_line(padded, taps, plane, column):
+    by_shift = [None, None, None]
+    for a in range(3):
+        for d in range(3):
+            window = padded[plane + a, column + d].astype(jnp.float32)
+            for b in range(3):
+                tap = (a * 3 + b) * 3 + d
+                term = taps[tap : tap + 1] * window
+                by_shift[b] = term if by_shift[b] is None else by_shift[b] + term
+    return shift_rows(by_shift[0], 1) + by_shift[1] + shift_rows(by_shift[2], -1)
+
+
+def put_tiles(target, matrix):
+    rows = matrix.shape[0] // 16
+    for column in range(matrix.shape[1] // 128):
+        target[column * rows : (column + 1) * rows] = matrix[
+            :, column * 128 : (column + 1) * 128
+        ].reshape(rows, 16, 128)
+
+
+def mlp_kernel(
+    padded, upstream, taps, up_weight, down_weight, block_out, grad_mixed, up_tiles, down_tiles,
+    mixed, normed, hidden, grad_pre
+):
+    planes, part_z, length, width = upstream.shape
+    for line in range(planes * part_z):
+        plane, column = line // part_z, line % part_z
+        rows = pl.ds(line * length, length)
+        centre = padded[plane + 1, column + 1].astype(jnp.float32)
+        mixed[rows] = (centre + conv_line(padded, taps, plane, column)).astype(jnp.bfloat16)
+    group = min(2, part_z)
+    for start in range(0, planes * part_z, group):
+        plane, columns = start // part_z, pl.ds(start % part_z, group)
+        rows = pl.ds(start * length, group * length)
+        mixed_wide = mixed[rows].astype(jnp.float32)
+        normal, inverse = norm_rows(mixed_wide)
+        normed[rows] = normal.astype(jnp.bfloat16)
+        pre_act = dot(normed[rows], up_weight[...])
+        square = pre_act * pre_act
+        tangent = jnp.tanh(GELU_SLOPE * (pre_act + GELU_CUBIC * square * pre_act))
+        hidden[rows] = (0.5 * pre_act * (1.0 + tangent)).astype(jnp.bfloat16)
+        slope = 0.5 * (1.0 + tangent) + 0.5 * pre_act * (1.0 - tangent * tangent) * GELU_SLOPE * (
+            1.0 + 3.0 * GELU_CUBIC * square
+        )
+        above = upstream[plane, columns].reshape(group * length, width)
+        grad_hidden = dot(above, down_weight[...], 1, 1).astype(jnp.bfloat16)
+        grad_pre[rows] = (grad_hidden.astype(jnp.float32) * slope).astype(jnp.bfloat16)
+        block_out[plane, columns] = (
+            (mixed_wide + dot(hidden[rows], down_weight[...]))
+            .astype(jnp.bfloat16)
+            .reshape(group, length, width)
+        )
+        grad_normed = dot(grad_pre[rows], up_weight[...], 1, 1)
+        grad_mixed[plane, columns] = (
+            (above.astype(jnp.float32) + norm_rows_back(grad_normed, normal, inverse))
+            .astype(jnp.bfloat16)
+            .reshape(group, length, width)
+        )
+    put_tiles(up_tiles, dot(normed[...], grad_pre[...], 0, 0))
+    put_tiles(down_tiles, dot(upstream[...].reshape(mixed.shape), hidden[...], 0, 0))
+
+
+def feed_forward(padded_value, upstream, conv_kernel, up_weight, down_weight):
+    width, hidden_width = up_weight.shape
+    count = upstream.size // width
+    tiles = wide(width * hidden_width // 2048, 16, 128)
+    return single(
+        mlp_kernel,
+        "feed_forward",
+        (low(*upstream.shape), low(*upstream.shape), tiles, tiles),
+        [
+            pltpu.VMEM((count, width), jnp.bfloat16),
+            pltpu.VMEM((count, width), jnp.bfloat16),
+            pltpu.VMEM((count, hidden_width), jnp.bfloat16),
+            pltpu.VMEM((count, hidden_width), jnp.bfloat16),
+        ],
+        padded_value,
+        upstream,
+        conv_kernel.reshape(27, width),
+        up_weight,
+        down_weight,
+    )
+
+
+def backward_kernel(
+    padded_value, padded_grad, tokens, query, key, value, attended, taps, qkv_weight, out_weight,
+    mask, token_gradient, joint_tiles, tap_tiles, grad_value, above, grad_query, grad_key, grad_low_value,
+    tap_sums
+):
+    planes, part_z, length, width = tokens.shape
+    lines = planes * part_z
+    tap_sums[...] = jnp.zeros_like(tap_sums)
+    for line in range(lines):
+        plane, column = line // part_z, line % part_z
+        rows = pl.ds(line * length, length)
+        centre = padded_grad[plane + 1, column + 1].astype(jnp.float32)
+        grad_value[rows] = (centre + conv_line(padded_grad, taps, plane, column)).astype(jnp.bfloat16)
+        shifted = (shift_rows(centre, -1), centre, shift_rows(centre, 1))
+        for a in range(3):
+            for d in range(3):
+                window = padded_value[plane + a, column + d].astype(jnp.float32)
+                for b in range(3):
+                    product = (shifted[b] * window).reshape(length // 8, 8, width)
+                    tap_sums[(a * 3 + b) * 3 + d] += jnp.sum(product, axis=0)
+    above[...] = dot(grad_value[...], out_weight[...], 1, 1).astype(jnp.bfloat16)
+    for line in range(lines):
+        rows = pl.ds(line * length, length)
+        query_vec, key_vec = query[rows].astype(jnp.float32), key[rows].astype(jnp.float32)
+        query_scale, key_scale, query_stack, key_unit, probs, factor = line_probs(
+            query_vec, key_vec, mask[...]
+        )
+        grad_stack = stack_heads(above[rows].astype(jnp.float32)).astype(jnp.bfloat16)
+        grad_probs = dot(grad_stack, value[rows], 1, 1)
+        grad_scores = probs * (grad_probs - jnp.sum(grad_probs * probs, axis=-1, keepdims=True))
+        grad_low = (factor * grad_scores).astype(jnp.bfloat16)
+        grad_low_value[rows] = dot(probs.astype(jnp.bfloat16), grad_stack, 0, 0).astype(jnp.bfloat16)
+        grad_qunit = unstack_heads(dot(grad_low, key_unit))
+        grad_kunit = dot(grad_low, query_stack, 0, 0)
+        grad_query[rows] = unit_back(grad_qunit, query_vec, query_scale).astype(jnp.bfloat16)
+        grad_key[rows] = unit_back(grad_kunit, key_vec, key_scale).astype(jnp.bfloat16)
+    normal, inverse = norm_rows(tokens[...].reshape(lines * length, width).astype(jnp.float32))
     normed = normal.astype(jnp.bfloat16)
-    qkv_rows = project(normed, qkv_weight).astype(jnp.bfloat16)
-    parts = attention_parts(qkv_rows, mask_full, HEADS)
-    width = token_lines.shape[-1]
-    value_heads = split_heads(qkv_rows[..., 2 * width :], HEADS)
-    probs_low = parts[6].astype(jnp.bfloat16)
-    attended = join_heads(head_product("abhij,abjhd->abihd", probs_low, value_heads)).astype(
-        jnp.bfloat16
-    )
-    value_field = (token_wide + project(attended, out_weight)).astype(jnp.bfloat16)
-    return value_field, (qkv_rows, attended)
-
-
-def conv_apply(padded, kernel_taps):
-    grown = jnp.concatenate([padded[:, :, -1:], padded, padded[:, :, :1]], axis=2)
-    extent_x, extent_z, extent_y = padded.shape[0] - 2, padded.shape[1] - 2, padded.shape[2]
-    summed = jnp.zeros((extent_x, extent_z, extent_y, padded.shape[3]), jnp.float32)
-    for a in range(3):
-        for b in range(3):
-            for d in range(3):
-                window = grown[a : a + extent_x, d : d + extent_z, b : b + extent_y]
-                summed = summed + kernel_taps[a, b, d] * window.astype(jnp.float32)
-    return summed
-
-
-def kernel_grad(padded, upstream):
-    grown = jnp.concatenate([padded[:, :, -1:], padded, padded[:, :, :1]], axis=2)
-    extent_x, extent_z, extent_y, channels = upstream.shape
-    upstream_wide = upstream.astype(jnp.float32)
-    pieces = []
-    for a in range(3):
-        for b in range(3):
-            for d in range(3):
-                window = grown[a : a + extent_x, d : d + extent_z, b : b + extent_y]
-                pieces.append(jnp.sum(window.astype(jnp.float32) * upstream_wide, axis=(0, 1, 2)))
-    return jnp.stack(pieces)
-
-
-def feed_forward(padded_value, upstream, conv_kernel, up_weight, down_weight):
-    value_field = padded_value[1:-1, 1:-1]
-    mixed_field = (value_field.astype(jnp.float32) + conv_apply(padded_value, conv_kernel)).astype(
-        jnp.bfloat16
-    )
-    mixed_wide = mixed_field.astype(jnp.float32)
-    normal, inverse = norm_rows(mixed_wide)
-    normed = normal.astype(jnp.bfloat16)
-    pre_act = project(normed, up_weight)
-    hidden = gelu_value(pre_act).astype(jnp.bfloat16)
-    block_out = (mixed_wide + project(hidden, down_weight)).astype(jnp.bfloat16)
-    grad_hidden = project_back(upstream, down_weight).astype(jnp.bfloat16)
-    part_down = contract(upstream, hidden)
-    grad_pre = (grad_hidden.astype(jnp.float32) * gelu_slope(pre_act)).astype(jnp.bfloat16)
-    part_up = contract(normed, grad_pre)
-    grad_normed = project_back(grad_pre, up_weight)
-    grad_mixed = (
-        upstream.astype(jnp.float32) + norm_rows_back(grad_normed, normal, inverse)
-    ).astype(jnp.bfloat16)
-    return (block_out, grad_mixed, part_up, part_down)
+    grad_normed, parts = 0.0, []
+    for piece, grad in enumerate((grad_query, grad_key, grad_low_value)):
+        weight = qkv_weight[:, piece * width : (piece + 1) * width]
+        grad_normed = grad_normed + dot(grad[...], weight, 1, 1)
+        parts.append(dot(normed, grad[...], 0, 0))
+    parts.append(dot(attended[...], grad_value[...], 0, 0))
+    put_tiles(joint_tiles, jnp.concatenate(parts, axis=1))
+    upstream = grad_normed.astype(jnp.bfloat16).astype(jnp.float32)
+    token_gradient[...] = (
+        (grad_value[...].astype(jnp.float32) + norm_rows_back(upstream, normal, inverse))
+        .astype(jnp.bfloat16)
+        .reshape(token_gradient.shape)
+    )
+    tap_tiles[...] = jnp.sum(tap_sums[...], axis=1)
 
 
 def attention_backward(
     token_lines, kept, padded_value, padded_grad, conv_kernel, qkv_weight, out_weight, mask_full
 ):
-    qkv_rows, attended = kept
-    grad_mixed = padded_grad[1:-1, 1:-1]
-    grad_value = (
-        grad_mixed.astype(jnp.float32) + conv_apply(padded_grad, conv_kernel[::-1, ::-1, ::-1])
-    ).astype(jnp.bfloat16)
-    part_kernel = kernel_grad(padded_value, grad_mixed)
-    upstream = project_back(grad_value, out_weight).astype(jnp.bfloat16)
-    part_out = contract(attended, grad_value)
-    query_vec, key_vec, query_scale, key_scale, query_unit, key_unit, attn_probs, factor = (
-        attention_parts(qkv_rows, mask_full, HEADS)
-    )
     width = token_lines.shape[-1]
-    value_heads = split_heads(qkv_rows[..., 2 * width :], HEADS)
-    grad_heads = split_heads(upstream, HEADS)
-    probs_low = attn_probs.astype(jnp.bfloat16)
-    grad_probs = head_product("abihd,abjhd->abhij", grad_heads, value_heads)
-    grad_values = head_product("abhij,abihd->abjhd", probs_low, grad_heads)
-    grad_scores = attn_probs * (
-        grad_probs - jnp.sum(grad_probs * attn_probs, axis=-1, keepdims=True)
-    )
-    grad_low = (factor * grad_scores).astype(jnp.bfloat16)
-    grad_qunit = join_heads(
-        head_product("abhij,abjhd->abihd", grad_low, split_heads(key_unit, HEADS))
-    )
-    grad_kunit = join_heads(
-        head_product("abhij,abihd->abjhd", grad_low, split_heads(query_unit, HEADS))
-    )
-    grad_query = unit_back(grad_qunit, query_vec, query_scale).astype(jnp.bfloat16)
-    grad_key = unit_back(grad_kunit, key_vec, key_scale).astype(jnp.bfloat16)
-    grad_qkv = jnp.concatenate(
-        [grad_query, grad_key, join_heads(grad_values).astype(jnp.bfloat16)], axis=-1
-    )
-    normal, inverse = norm_rows(token_lines.astype(jnp.float32))
-    grad_normed = project_back(grad_qkv, qkv_weight).astype(jnp.bfloat16)
-    part_qkv = contract(normal.astype(jnp.bfloat16), grad_qkv)
-    token_gradient = (
-        grad_value.astype(jnp.float32)
-        + norm_rows_back(grad_normed.astype(jnp.float32), normal, inverse)
-    ).astype(jnp.bfloat16)
-    return token_gradient, jnp.concatenate([part_qkv, part_out], axis=1), part_kernel
+    count = token_lines.size // width
+    return single(
+        backward_kernel,
+        "attention_backward",
+        (low(*token_lines.shape), wide(4 * width * width // 2048, 16, 128), wide(27, width)),
+        [pltpu.VMEM((count, width), jnp.bfloat16)] * 5 + [pltpu.VMEM((27, 8, width), jnp.float32)],
+        padded_value,
+        padded_grad,
+        token_lines,
+        *kept,
+        conv_kernel[::-1, ::-1, ::-1].reshape(27, width),
+        qkv_weight,
+        out_weight,
+        stacked_mask(mask_full),
+    )
 
 
 def local(tokens, qkv_weight, out_weight, conv_kernel, up_weight, down_weight, band_mask, grad_out):
@@ -510,7 +581,7 @@
         token_lines, kept, padded_value, padded_grad, conv_kernel, qkv_weight, out_weight, mask_full
     )
     hidden_width = up_weight.shape[1]
-    pieces = [tiles_of(part_up), tiles_of(part_down), tiles_of(part_qkv_out)]
+    pieces = [part_up, part_down, part_qkv_out]
     kernel_flat = part_kernel.reshape(-1)
     kernel_tiles = -(-kernel_flat.shape[0] // 2048)
     used = sum(piece.shape[0] for piece in pieces)

time: 178 us -> 135 us (0.76)
  matrix products: 28.1 us -> 0 us
  other arithmetic: 28.7 us -> 2.03 us
  Pallas kernels: 88.1 us -> 102 us
    dot_general x18 -> x0, matrix products: 28.1 us -> none  [the longest x6 16.5 us: head_product(): jnp.einsum(einsum_form, left_side, right_side, preferred_element_type=jnp...]
    reduce_sum x10 -> x0, other arithmetic: 14.3 us -> none  [the longest x2 7.25 us: norm_rows(): centred = values - jnp.mean(values, axis=-1, keepdims=True)]
    pallas_call x0 -> x3, Pallas kernels: none -> 13.4 us  [single(): pl.pallas_call(body, out_shape=outs, in_specs=[VMEM] * len(operands), out...]
    convert_element_type x5 -> x0, other arithmetic: 5.87 us -> none  [the longest x1 3.01 us: attention_backward(): grad_value = (grad_mixed.astype(jnp.float32) + conv_apply(padded_grad, co...]
    unnamed x199 -> x46, local copies, waits for them, and re-layouts: 6.24 us -> 12.1 us
    reshape x6 -> x5, local copies, waits for them, and re-layouts: 5.5 us -> 1.87 us  [the longest x3 1.07 us: from_tiles(): tiles.reshape(columns // 128, rows, 128).transpose(1, 0, 2)]
    reshape x1 -> x0, other arithmetic: 3.44 us -> none  [from_lines(): lines.reshape(planes, part_z, -1, part_y, width).transpose(2, 0, 3, 1, 4)]
    div x9 -> x0, other arithmetic: 3.28 us -> none  [the longest x1 3.25 us: attention_parts(): attn_probs = weights / jnp.sum(weights, axis=-1, keepdims=True)]
where the time goes in v2:
time: 135 us; the launch traced here: 134 us
  Pallas kernels  102 us (76%)
  local copies, waits for them, and re-layouts  29.5 us (22%)
  other arithmetic  2.03 us (2%)
    pallas_call x1, Pallas kernels, reduce_and_swap(): pl.pallas_call(functools.partial(reduce_kernel, count_y, count_z), out_sh...  43.7 us
    pallas_call x2, Pallas kernels, halo(): pl.pallas_call(functools.partial(halo_kernel, count_y, count_z), out_shap...  27.9 us
    pallas_call x1, Pallas kernels, swap_lines(): pl.pallas_call(functools.partial(swap_kernel, count), out_shape=(shape, s...  16.5 us
    pallas_call x3, Pallas kernels, single(): pl.pallas_call(body, out_shape=outs, in_specs=[VMEM] * len(operands), out...  13.4 us
    unnamed x46, local copies, waits for them, and re-layouts  12.1 us

profile of v2, /device:TPU:0, one launch (start us, length us, event | category | flops | bytes accessed | tf_op | source)
XLA Modules:
  0.0 134.1 jit_solution(10292172490231578098)
XLA Ops:
  2.1 0.8 rev.3
  3.2 1.9 %reshape.97.first_in = bf16[8,64,192]{2,1,0:T(8,128)(2,1)} reshape(bf16[16,8,4,192]{3,2,1,0:T(4,128)(2,1)} %param.8) | data formatting | bytes 393216 | tf_op jit(solution)/shard_map/reshape | solution.py:570
  5.1 1.9 %reshape.98.second_in = bf16[8,64,192]{2,1,0:T(8,128)(2,1)} reshape(bf16[16,8,4,192]{3,2,1,0:T(4,128)(2,1)} %param.15) | data formatting | bytes 393216 | tf_op jit(solution)/shard_map/reshape | solution.py:570
  6.9 16.5 %swap_lines.1 = (bf16[8,64,192]{2,1,0:T(8,128)(2,1)}, bf16[8,64,192]{2,1,0:T(8,128)(2,1)}) custom-call(bf16[8,64,192]{2,1,0:T(8,128)(2,1)} %reshape.97.first_in, bf16[8,64,192]{2,1,0:T(8,128)(2,1)} %reshape.98.second_in), custom_call_target="tpu_custom_call" | custom-call | tf_op jit(solution)/shard_map/swap_lines/pallas_call | solution.py:95
  23.4 1.0 reshape.99
  24.5 1.0 reshape.101
  25.8 2.0 %attention_forward.1 = (bf16[2,4,64,192]{3,2,1,0:T(8,128)(2,1)S(1)}, bf16[512,192]{1,0:T(8,128)(2,1)S(1)}, bf16[512,192]{1,0:T(8,128)(2,1)S(1)}, bf16[512,192]{1,0:T(8,128)(2,1)S(1)}, bf16[512,192]{1,0:T(8,128)(2,1)S(1)}) custom-call(bf16[2,4,64,192]{3,2,1,0:T(8,128)(2,1)S(1)} %bitcast.39, bf16[192,576]{1,0:T(8,128)(2,1)S(1)} %copy-done.3, ...), custom_call_target="tpu_custom_call" | custom-call | tf_op jit(solution)/shard_map/attention_forward/pallas_call | solution.py:354
  31.3 14.5 %halo1.1.padded.padded_value = bf16[4,6,64,192]{3,2,1,0:T(8,128)(2,1)} custom-call(bf16[2,4,64,192]{3,2,1,0:T(8,128)(2,1)} %copy-done.12), custom_call_target="tpu_custom_call" | custom-call | tf_op jit(solution)/shard_map/halo1/pallas_call | solution.py:175
  45.8 1.1 copy-done
  46.9 1.0 copy-done.7
  47.9 3.6 %feed_forward.1 = (bf16[2,4,64,192]{3,2,1,0:T(8,128)(2,1)S(1)}, bf16[2,4,64,192]{3,2,1,0:T(8,128)(2,1)S(1)}, f32[72,16,128]{2,1,0:T(8,128)S(1)}, f32[72,16,128]{2,1,0:T(8,128)S(1)}) custom-call(bf16[4,6,64,192]{3,2,1,0:T(8,128)(2,1)S(1)} %copy-done, bf16[2,4,64,192]{3,2,1,0:T(8,128)(2,1)S(1)} %bitcast.43, f32[27,192]{1,0:T(8,128)S(1)} %reshape.103.taps, ...), custom_call_target="tpu_custom_call" | custom-call | tf_op jit(solution)/shard_map/feed_forward/pallas_call | solution.py:354
  51.5 0.9 copy.43
  52.5 1.1 reshape.108.first_in
  53.6 13.5 %halo2.1.padded_grad = bf16[4,6,64,192]{3,2,1,0:T(8,128)(2,1)} custom-call(bf16[2,4,64,192]{3,2,1,0:T(8,128)(2,1)} %copy-done.11), custom_call_target="tpu_custom_call" | custom-call | tf_op jit(solution)/shard_map/halo2/pallas_call | solution.py:175
  67.1 1.1 copy-done.2
  68.2 0.9 copy-done.16
  69.2 0.9 copy-done.18
  70.1 0.9 copy-done.20
  71.1 7.8 %attention_backward.1 = (bf16[2,4,64,192]{3,2,1,0:T(8,128)(2,1)S(1)}, f32[72,16,128]{2,1,0:T(8,128)S(1)}, f32[27,192]{1,0:T(8,128)S(1)}) custom-call(bf16[4,6,64,192]{3,2,1,0:T(8,128)(2,1)S(1)} %copy-done.1, bf16[4,6,64,192]{3,2,1,0:T(8,128)(2,1)S(1)} %copy-done.2, bf16[2,4,64,192]{3,2,1,0:T(8,128)(2,1)S(1)} %bitcast.40, bf16[512,192]{1,0:T(8,128)(2,1)S(1)} %copy-done.14, ...), custom_call_target="tpu_custom_call" | custom-call | tf_op jit(solution)/shard_map/attention_backward/pallas_call | solution.py:354
  80.5 1.2 pad_maximum_fusion.parts
  82.1 43.7 %reduce_and_swap.1 = (bf16[224,16,128]{2,1,0:T(8,128)(2,1)S(1)}, bf16[8,64,192]{2,1,0:T(8,128)(2,1)S(1)}, bf16[8,64,192]{2,1,0:T(8,128)(2,1)S(1)}) custom-call(f32[224,16,128]{2,1,0:T(8,128)S(1)} %pad_maximum_fusion.parts, bf16[8,64,192]{2,1,0:T(8,128)(2,1)S(1)} %reshape.108.first_in, bf16[8,64,192]{2,1,0:T(8,128)(2,1)S(1)} %reshape.110.second_in), custom_call_target="tpu_custom_call" | custom-call | tf_op jit(solution)/shard_map/reduce_and_swap/pallas_call | solution.py:260
  126.6 1.7 %reshape.111 = bf16[16,8,4,192]{3,2,1,0:T(4,128)(2,1)} reshape(bf16[8,64,192]{2,1,0:T(8,128)(2,1)} %copy-done.10) | data formatting | bytes 393216 | tf_op jit(solution)/shard_map/reshape | solution.py:603
  130.8 1.3 bitcast_bitcast_fusion
  133.3 0.8 slice.29
  (62 shorter events, 11.9 us)
Async XLA Ops:
  3.2 22.4 %copy-start.21 = (bf16[768,192]{0,1:T(8,128)(2,1)S(1)}, bf16[768,192]{0,1:T(8,128)(2,1)}, u32[]{:S(2)}) copy-start(bf16[768,192]{0,1:T(8,128)(2,1)} %param.13) | copy-start | bytes 884740
  5.0 20.7 %copy-start.3 = (bf16[192,576]{1,0:T(8,128)(2,1)S(1)}, bf16[192,576]{1,0:T(8,128)(2,1)}, u32[]{:S(2)}) copy-start(bf16[192,576]{1,0:T(8,128)(2,1)} %qkv_weight.3) | copy-start | bytes 663556
  5.1 20.7 %copy-start.5 = (bf16[192,192]{1,0:T(8,128)(2,1)S(1)}, bf16[192,192]{1,0:T(8,128)(2,1)}, u32[]{:S(2)}) copy-start(bf16[192,192]{1,0:T(8,128)(2,1)} %out_weight.3) | copy-start | bytes 221188
  27.8 0.7 copy-start.12
  28.5 0.7 copy-start.13
  29.2 0.7 copy-start.15
  29.9 0.7 copy-start.17
  30.6 0.7 copy-start.19
  45.8 1.1 copy-start
  46.9 1.0 copy-start.7
  47.9 19.2 %copy-start.1 = (bf16[4,6,64,192]{3,2,1,0:T(8,128)(2,1)S(1)}, bf16[4,6,64,192]{3,2,1,0:T(8,128)(2,1)}, u32[]{:S(2)}) copy-start(bf16[4,6,64,192]{3,2,1,0:T(8,128)(2,1)} %halo1.1.padded.padded_value) | copy-start | bytes 1769476
  51.5 1.0 copy-start.11
  51.5 15.6 %copy-start.6 = (bf16[192,192]{1,0:T(8,128)(2,1)S(1)}, bf16[192,192]{1,0:T(8,128)(2,1)}, u32[]{:S(2)}) copy-start(bf16[192,192]{1,0:T(8,128)(2,1)} %out_weight.3) | copy-start | bytes 221188
  51.5 15.6 %copy-start.14 = (bf16[512,192]{1,0:T(8,128)(2,1)S(1)}, bf16[512,192]{1,0:T(8,128)(2,1)}, u32[]{:S(2)}) copy-start(bf16[512,192]{1,0:T(8,128)(2,1)} %copy-done.13) | copy-start | bytes 589828
  67.1 1.1 copy-start.2
  68.2 0.9 copy-start.16
  69.2 0.9 copy-start.18
  70.1 0.9 copy-start.20
  78.9 0.8 copy-start.4
  79.7 0.7 copy-start.8
  80.5 1.2 copy-start.9
  125.9 0.7 copy-start.10

commit v3 on v2

--- a/solution.py
+++ b/solution.py
@@ -58,7 +58,11 @@
     return [(lax.rem(me_y + k, count), me_z) for k in range(1, count)]
 
 
-def swap_copies(count, pairs, send_sem, recv_sem):
+def place_of(index):
+    return index + (1 - 2 * lax.rem(index, 2)) * lax.rem(index // 2, 2)
+
+
+def swap_copies(count, pairs, send_sem, recv_sem, inward):
     me_y, me_z = lax.axis_index("gy"), lax.axis_index("gz")
     copies = []
     for k in range(1, count):
@@ -66,8 +70,8 @@
         for a, (source, target) in enumerate(pairs):
             copies.append(
                 pltpu.make_async_remote_copy(
-                    src_ref=source.at[peer],
-                    dst_ref=target.at[me_y],
+                    src_ref=source.at[place_of(peer) if inward else peer],
+                    dst_ref=target.at[me_y if inward else place_of(me_y)],
                     send_sem=send_sem.at[a, k],
                     recv_sem=recv_sem.at[a, k],
                     device_id=(peer, me_z),
@@ -80,12 +84,12 @@
 def swap_kernel(count, first_in, second_in, first_out, second_out, send_sem, recv_sem):
     greet(line_peers(count))
     pairs = ((first_in, first_out), (second_in, second_out))
-    copies = swap_copies(count, pairs, send_sem, recv_sem)
+    copies = swap_copies(count, pairs, send_sem, recv_sem, True)
     for copy in copies:
         copy.start()
     me_y = lax.axis_index("gy")
     for source, target in pairs:
-        target[me_y] = source[me_y]
+        target[me_y] = source[place_of(me_y)]
     for copy in copies:
         copy.wait()
 
@@ -108,7 +112,7 @@
 
 
 def halo_kernel(count_y, count_z, cells, padded, send_sem, recv_sem):
-    me_y, me_z = lax.axis_index("gy"), lax.axis_index("gz")
+    me_y, me_z = place_of(lax.axis_index("gy")), lax.axis_index("gz")
     extent_x, extent_z = cells.shape[0], cells.shape[1]
     steps = [(dx, dz) for dx in (-1, 0, 1) for dz in (-1, 0, 1) if (dx, dz) != (0, 0)]
     barrier = pltpu.get_barrier_semaphore()
@@ -122,7 +126,7 @@
             pl.when(me_y > 0)(action)
 
     def place(dx, dz):
-        return (me_y + dx, lax.rem(me_z + dz + count_z, count_z))
+        return (place_of(me_y + dx), lax.rem(me_z + dz + count_z, count_z))
 
     def greet_one(dx, dz):
         pl.semaphore_signal(barrier, inc=1, device_id=place(dx, dz), device_id_type=MESH)
@@ -183,96 +187,134 @@
     )(cells)
 
 
-def bits_of(count_y, count_z):
-    levels = []
-    for axis, count in (("gz", count_z), ("gy", count_y)):
-        bit = 1
-        while bit < count:
-            levels.append((axis, bit))
-            bit *= 2
-    return levels
-
-
-def reduce_kernel(count_y, count_z, parts, first_in, second_in, sums, first_out, second_out, *scratch):
+def bits_of(count):
+    return [1 << level for level in range(count.bit_length() - 1)]
+
+
+def reduce_kernel(
+    count_y, count_z, chains, parts, first_in, second_in, sums, first_out, second_out, *scratch
+):
     swap_send, swap_recv, send_sem, recv_sem, total = scratch[:5]
-    stages = bits_of(count_y, count_z)
-    depth = len(stages)
-    outgoing, incoming = scratch[5 : 5 + depth], scratch[5 + depth : 5 + 2 * depth]
-    me = {"gy": lax.axis_index("gy"), "gz": lax.axis_index("gz")}
-    bit_values, partners = [], []
-    for axis, bit in stages:
-        value = lax.rem(me[axis] // bit, 2)
-        moved = me[axis] + bit * (1 - 2 * value)
-        bit_values.append(value)
-        partners.append((moved, me["gz"]) if axis == "gy" else (me["gy"], moved))
-    greet(line_peers(count_y) + [partner for (axis, _), partner in zip(stages, partners) if axis == "gz"])
+    buffers = scratch[5:]
+    bits = bits_of(count_z)
+    depth = len(bits)
+    me_y, me_z = lax.axis_index("gy"), lax.axis_index("gz")
+    values = [lax.rem(me_z // bit, 2) for bit in bits]
+    partners = [(me_y, me_z + bit * (1 - 2 * value)) for bit, value in zip(bits, values)]
+    greet(line_peers(count_y) + partners)
     pairs = ((first_in, first_out), (second_in, second_out))
-    copies = swap_copies(count_y, pairs, swap_send, swap_recv)
-    for copy in copies:
-        copy.start()
-    for source, target in pairs:
-        target[me["gy"]] = source[me["gy"]]
-    held, size = parts, parts.shape[0]
-    base, bases = 0, []
-    for level in range(depth):
-        half = size // 2
-        keep = base + bit_values[level] * half
-        away = base + (1 - bit_values[level]) * half
-        outgoing[level][...] = held[pl.ds(away, half)].astype(jnp.bfloat16)
+    copies = swap_copies(count_y, pairs, swap_send, swap_recv, False)
+
+    def send(source, target, chain, slot, peer):
         copy = pltpu.make_async_remote_copy(
-            src_ref=outgoing[level],
-            dst_ref=incoming[level],
-            send_sem=send_sem.at[level],
-            recv_sem=recv_sem.at[level],
-            device_id=partners[level],
+            src_ref=source,
+            dst_ref=target,
+            send_sem=send_sem.at[chain, slot],
+            recv_sem=recv_sem.at[chain, slot],
+            device_id=peer,
             device_id_type=MESH,
         )
         copy.start()
-        copy.wait()
-        total[pl.ds(keep, half)] = held[pl.ds(keep, half)] + incoming[level][...].astype(jnp.float32)
-        held, base, size = total, keep, half
-        bases.append(keep)
-    sums[pl.ds(base, size)] = total[pl.ds(base, size)].astype(jnp.bfloat16)
-    for level in range(depth - 1, -1, -1):
-        span = pl.ds(bases[level], size)
-        copy = pltpu.make_async_remote_copy(
-            src_ref=sums.at[span],
-            dst_ref=sums.at[span],
-            send_sem=send_sem.at[depth + level],
-            recv_sem=recv_sem.at[depth + level],
-            device_id=partners[level],
-            device_id_type=MESH,
-        )
-        copy.start()
-        copy.wait()
-        size *= 2
+        return copy
+
+    def run_chain(chain):
+        base, size = chains[chain]
+        mine = buffers[chain * (2 * depth + 2) : (chain + 1) * (2 * depth + 2)]
+        outgoing, incoming = mine[: depth + 1], mine[depth + 1 :]
+        held, bases = parts, []
+        for level in range(depth):
+            half = size // 2
+            keep = base + values[level] * half
+            away = base + (1 - values[level]) * half
+            outgoing[level][...] = held[pl.ds(away, half)].astype(jnp.bfloat16)
+            copy = send(outgoing[level], incoming[level], chain, level, partners[level])
+            yield
+            copy.wait()
+            total[pl.ds(keep, half)] = held[pl.ds(keep, half)] + incoming[level][...].astype(
+                jnp.float32
+            )
+            held, base, size = total, keep, half
+            bases.append(keep)
+        part = size // count_y
+        outgoing[depth][...] = held[pl.ds(base, size)].astype(jnp.bfloat16)
+        spread = []
+        for k in range(1, count_y):
+            peer = lax.rem(me_y + k, count_y)
+            source = outgoing[depth].at[pl.ds(peer * part, part)]
+            spread.append(
+                send(source, incoming[depth].at[k], chain, 2 * depth + k, (peer, me_z))
+            )
+        yield
+        own = pl.ds(base + me_y * part, part)
+        summed = held[own]
+        for k, copy in enumerate(spread):
+            copy.wait()
+            summed = summed + incoming[depth][k + 1].astype(jnp.float32)
+        sums[own] = summed.astype(jnp.bfloat16)
+        spread = []
+        for k in range(1, count_y):
+            peer = lax.rem(me_y + k, count_y)
+            spread.append(
+                send(sums.at[own], sums.at[own], chain, 2 * depth + count_y + k, (peer, me_z))
+            )
+        yield
+        for copy in spread:
+            copy.wait()
+        for level in range(depth - 1, -1, -1):
+            span = pl.ds(bases[level], size)
+            copy = send(sums.at[span], sums.at[span], chain, depth + level, partners[level])
+            yield
+            copy.wait()
+            size *= 2
+
+    running = [run_chain(chain) for chain in range(len(chains))]
+    first_round = True
+    while running:
+        still = []
+        for work in running:
+            if next(work, "done") is None:
+                still.append(work)
+        running = still
+        if first_round:
+            for copy in copies:
+                copy.start()
+            for source, target in pairs:
+                target[place_of(me_y)] = source[me_y]
+            first_round = False
     for copy in copies:
         copy.wait()
 
 
 def reduce_and_swap(parts, first, second, count_y, count_z):
-    depth = len(bits_of(count_y, count_z))
+    depth = len(bits_of(count_z))
     shape = jax.ShapeDtypeStruct(first.shape, first.dtype)
-    halves = [
-        pltpu.VMEM((parts.shape[0] >> (level + 1),) + parts.shape[1:], jnp.bfloat16)
-        for level in range(depth)
-    ]
+    units = parts.shape[0] // (count_y * count_z)
+    chain_count = min(3, units)
+    cuts = [i * units // chain_count * count_y * count_z for i in range(chain_count + 1)]
+    chains = [(low_cut, high_cut - low_cut) for low_cut, high_cut in zip(cuts, cuts[1:])]
+    tile = parts.shape[1:]
+    buffers = []
+    for _, size in chains:
+        halves = [(size >> (level + 1),) + tile for level in range(depth)]
+        last = size >> depth
+        shapes = halves + [(last,) + tile] + halves + [(count_y, last // count_y) + tile]
+        buffers += [pltpu.VMEM(entry, jnp.bfloat16) for entry in shapes]
+    slots = (chain_count, 2 * depth + 2 * count_y)
     return pl.pallas_call(
-        functools.partial(reduce_kernel, count_y, count_z),
+        functools.partial(reduce_kernel, count_y, count_z, chains),
         out_shape=(jax.ShapeDtypeStruct(parts.shape, jnp.bfloat16), shape, shape),
         in_specs=[VMEM, VMEM, VMEM],
         out_specs=(VMEM, VMEM, VMEM),
         scratch_shapes=[
             pltpu.SemaphoreType.DMA((2, count_y)),
             pltpu.SemaphoreType.DMA((2, count_y)),
-            pltpu.SemaphoreType.DMA((2 * depth,)),
-            pltpu.SemaphoreType.DMA((2 * depth,)),
+            pltpu.SemaphoreType.DMA(slots),
+            pltpu.SemaphoreType.DMA(slots),
             pltpu.VMEM(parts.shape, jnp.float32),
         ]
-        + halves
-        + halves,
+        + buffers,
         compiler_params=pltpu.CompilerParams(
-            collective_id=3, has_side_effects=True, vmem_limit_bytes=24 * 1024 * 1024
+            collective_id=3, has_side_effects=True, vmem_limit_bytes=60 * 1024 * 1024
         ),
         name="reduce_and_swap",
     )(parts, first, second)
@@ -357,7 +399,7 @@
         in_specs=[VMEM] * len(operands),
         out_specs=[VMEM] * len(outs),
         scratch_shapes=scratch,
-        compiler_params=pltpu.CompilerParams(vmem_limit_bytes=32 * 1024 * 1024),
+        compiler_params=pltpu.CompilerParams(vmem_limit_bytes=60 * 1024 * 1024),
         name=name,
     )(*operands)
 

time: 135 us -> 128 us (0.948)
  local copies, waits for them, and re-layouts: 29.5 us -> 24.1 us
  Pallas kernels: 102 us -> 97.5 us
  other arithmetic: 2.03 us -> 4.47 us
    unnamed x46 -> x10, local copies, waits for them, and re-layouts: 12.1 us -> 1.05 us
    pallas_call x3, Pallas kernels: 13.4 us -> 20.3 us  [single(): pl.pallas_call(body, out_shape=outs, in_specs=[VMEM] * len(operands), out...]
    pallas_call x1, Pallas kernels: 43.7 us -> 37.2 us  [reduce_and_swap(): pl.pallas_call(functools.partial(reduce_kernel, count_y, count_z, chains)...]
    pallas_call x2, Pallas kernels: 27.9 us -> 23.4 us  [halo(): pl.pallas_call(functools.partial(halo_kernel, count_y, count_z), out_shap...]
    reshape x4, local copies, waits for them, and re-layouts: 2.13 us -> 3.55 us  [to_lines(): swapped.reshape(-1, planes, part_y, part_z, width).transpose(1, 3, 0, 2, 4)]
where the time goes in v3:
time: 128 us; the launch traced here: 127 us
  Pallas kernels  97.5 us (76%)
  local copies, waits for them, and re-layouts  24.1 us (19%)
  other arithmetic  4.47 us (3%)
    pallas_call x1, Pallas kernels, reduce_and_swap(): pl.pallas_call(functools.partial(reduce_kernel, count_y, count_z, chains)...  37.2 us
    pallas_call x2, Pallas kernels, halo(): pl.pallas_call(functools.partial(halo_kernel, count_y, count_z), out_shap...  23.4 us
    pallas_call x3, Pallas kernels, single(): pl.pallas_call(body, out_shape=outs, in_specs=[VMEM] * len(operands), out...  20.3 us
    pallas_call x1, Pallas kernels, swap_lines(): pl.pallas_call(functools.partial(swap_kernel, count), out_shape=(shape, s...  16.5 us
    reshape x4, local copies, waits for them, and re-layouts, to_lines(): swapped.reshape(-1, planes, part_y, part_z, width).transpose(1, 3, 0, 2, 4)  3.55 us

profile of v3, /device:TPU:0, one launch (start us, length us, event | category | flops | bytes accessed | tf_op | source)
XLA Modules:
  0.0 126.9 jit_solution(12308946815670634508)
XLA Ops:
  1.3 1.4 %reshape.103.taps = f32[27,192]{1,0:T(8,128)} reshape(f32[3,3,3,192]{3,2,1,0:T(4,128)} %param.11) | data formatting | bytes 41472 | tf_op jit(solution)/shard_map/reshape | solution.py:518
  2.7 0.8 rev.3
  5.0 1.9 %reshape.97.first_in = bf16[8,64,192]{2,1,0:T(8,128)(2,1)} reshape(bf16[16,8,4,192]{3,2,1,0:T(4,128)(2,1)} %param.8) | data formatting | bytes 393216 | tf_op jit(solution)/shard_map/reshape | solution.py:612
  6.9 1.8 %reshape.98.second_in = bf16[8,64,192]{2,1,0:T(8,128)(2,1)} reshape(bf16[16,8,4,192]{3,2,1,0:T(4,128)(2,1)} %param.15) | data formatting | bytes 393216 | tf_op jit(solution)/shard_map/reshape | solution.py:612
  8.7 16.5 %swap_lines.1 = (bf16[8,64,192]{2,1,0:T(8,128)(2,1)}, bf16[8,64,192]{2,1,0:T(8,128)(2,1)}) custom-call(bf16[8,64,192]{2,1,0:T(8,128)(2,1)} %reshape.97.first_in, bf16[8,64,192]{2,1,0:T(8,128)(2,1)} %reshape.98.second_in), custom_call_target="tpu_custom_call" | custom-call | tf_op jit(solution)/shard_map/swap_lines/pallas_call | solution.py:99
  25.2 1.0 reshape.99
  27.0 1.0 reshape.101
  28.8 0.9 copy.25.down_weight
  29.7 3.9 %attention_forward.1 = (bf16[2,4,64,192]{3,2,1,0:T(8,128)(2,1)}, bf16[512,192]{1,0:T(8,128)(2,1)}, bf16[512,192]{1,0:T(8,128)(2,1)}, bf16[512,192]{1,0:T(8,128)(2,1)}, bf16[512,192]{1,0:T(8,128)(2,1)}) custom-call(bf16[2,4,64,192]{3,2,1,0:T(8,128)(2,1)} %bitcast.47, bf16[192,576]{1,0:T(8,128)(2,1)} %qkv_weight.3, bf16[192,192]{1,0:T(8,128)(2,1)} %out_weight.3, ...), custom_call_target="tpu_custom_call" | custom-call | tf_op jit(solution)/shard_map/attention_forward/pallas_call | solution.py:396
  33.6 13.5 %halo1.1.padded.padded_value = bf16[4,6,64,192]{3,2,1,0:T(8,128)(2,1)} custom-call(bf16[2,4,64,192]{3,2,1,0:T(8,128)(2,1)} %get-tuple-element.25.cells), custom_call_target="tpu_custom_call" | custom-call | tf_op jit(solution)/shard_map/halo1/pallas_call | solution.py:179
  47.1 5.9 %feed_forward.1 = (bf16[2,4,64,192]{3,2,1,0:T(8,128)(2,1)}, bf16[2,4,64,192]{3,2,1,0:T(8,128)(2,1)}, f32[72,16,128]{2,1,0:T(8,128)}, f32[72,16,128]{2,1,0:T(8,128)}) custom-call(bf16[4,6,64,192]{3,2,1,0:T(8,128)(2,1)} %halo1.1.padded.padded_value, bf16[2,4,64,192]{3,2,1,0:T(8,128)(2,1)} %bitcast.51, f32[27,192]{1,0:T(8,128)} %reshape.103.taps, ...), custom_call_target="tpu_custom_call" | custom-call | tf_op jit(solution)/shard_map/feed_forward/pallas_call | solution.py:396
  53.1 1.2 copy.43
  54.2 0.9 reshape.108.first_in
  55.1 9.9 %halo2.1.padded_grad = bf16[4,6,64,192]{3,2,1,0:T(8,128)(2,1)} custom-call(bf16[2,4,64,192]{3,2,1,0:T(8,128)(2,1)} %get-tuple-element.29.cells), custom_call_target="tpu_custom_call" | custom-call | tf_op jit(solution)/shard_map/halo2/pallas_call | solution.py:179
  65.1 10.5 %attention_backward.1 = (bf16[2,4,64,192]{3,2,1,0:T(8,128)(2,1)}, f32[72,16,128]{2,1,0:T(8,128)}, f32[27,192]{1,0:T(8,128)}) custom-call(bf16[4,6,64,192]{3,2,1,0:T(8,128)(2,1)} %halo1.1.padded.padded_value, bf16[4,6,64,192]{3,2,1,0:T(8,128)(2,1)} %halo2.1.padded_grad, bf16[2,4,64,192]{3,2,1,0:T(8,128)(2,1)} %bitcast.48, ...), custom_call_target="tpu_custom_call" | custom-call | tf_op jit(solution)/shard_map/attention_backward/pallas_call | solution.py:396
  75.5 0.8 reshape.105
  76.4 2.5 %pad_maximum_fusion.parts = f32[224,16,128]{2,1,0:T(8,128)} fusion(f32[8,16,128]{2,1,0:T(8,128)S(1)} %bitcast.54, f32[72,16,128]{2,1,0:T(8,128)} %get-tuple-element.34, f32[72,16,128]{2,1,0:T(8,128)S(1)} %copy-done.1, f32[72,16,128]{2,1,0:T(8,128)S(1)} %copy-done), kind=kLoop, calls=%fused_computation | loop fusion | flops 1376256 | bytes 3670016 | tf_op jit(solution)/shard_map/concatenate | solution.py:633
  79.1 0.9 reshape.110.second_in
  80.0 37.2 %reduce_and_swap.1 = (bf16[224,16,128]{2,1,0:T(8,128)(2,1)}, bf16[8,64,192]{2,1,0:T(8,128)(2,1)}, bf16[8,64,192]{2,1,0:T(8,128)(2,1)}) custom-call(f32[224,16,128]{2,1,0:T(8,128)} %pad_maximum_fusion.parts, bf16[8,64,192]{2,1,0:T(8,128)(2,1)} %reshape.108.first_in, bf16[8,64,192]{2,1,0:T(8,128)(2,1)} %reshape.110.second_in), custom_call_target="tpu_custom_call" | custom-call | tf_op jit(solution)/shard_map/reduce_and_swap/pallas_call | solution.py:303
  117.2 1.7 %reshape.111 = bf16[16,8,4,192]{3,2,1,0:T(4,128)(2,1)} reshape(bf16[8,64,192]{2,1,0:T(8,128)(2,1)} %get-tuple-element.38) | data formatting | bytes 393216 | tf_op jit(solution)/shard_map/reshape | solution.py:645
  119.0 1.7 %reshape.112 = bf16[16,8,4,192]{3,2,1,0:T(4,128)(2,1)} reshape(bf16[8,64,192]{2,1,0:T(8,128)(2,1)} %get-tuple-element.39) | data formatting | bytes 393216 | tf_op jit(solution)/shard_map/reshape | solution.py:646
  120.7 1.3 %convert_multiply_fusion = f32[224,16,128]{2,1,0:T(8,128)S(1)} fusion(bf16[224,16,128]{2,1,0:T(8,128)(2,1)} %get-tuple-element.40), kind=kLoop, calls=%fused_computation.1 | loop fusion | flops 917504 | bytes 2752512 | tf_op jit(solution)/shard_map/mul | solution.py:638
  123.6 1.3 bitcast_bitcast_fusion
  126.1 0.8 slice.29
  (26 shorter events, 6.7 us)
Async XLA Ops:
  5.0 23.7 %copy-start.2 = (bf16[768,192]{0,1:T(8,128)(2,1)S(1)}, bf16[768,192]{0,1:T(8,128)(2,1)}, u32[]{:S(2)}) copy-start(bf16[768,192]{0,1:T(8,128)(2,1)} %param.13) | copy-start | bytes 884740
  65.0 11.3 %copy-start = (f32[72,16,128]{2,1,0:T(8,128)S(1)}, f32[72,16,128]{2,1,0:T(8,128)}, u32[]{:S(2)}) copy-start(f32[72,16,128]{2,1,0:T(8,128)} %get-tuple-element.27) | copy-start | bytes 1769476
  65.0 11.3 %copy-start.1 = (f32[72,16,128]{2,1,0:T(8,128)S(1)}, f32[72,16,128]{2,1,0:T(8,128)}, u32[]{:S(2)}) copy-start(f32[72,16,128]{2,1,0:T(8,128)} %get-tuple-element.28) | copy-start | bytes 1769476
  76.4 2.5 %copy-start.3 = (bf16[2,4,64,192]{3,2,1,0:T(8,128)(2,1)S(1)}, bf16[2,4,64,192]{3,2,1,0:T(8,128)(2,1)}, u32[]{:S(2)}) copy-start(bf16[2,4,64,192]{3,2,1,0:T(8,128)(2,1)} %get-tuple-element.37) | copy-start | bytes 589828

commit v4 on v3

--- a/solution.py
+++ b/solution.py
@@ -314,7 +314,7 @@
         ]
         + buffers,
         compiler_params=pltpu.CompilerParams(
-            collective_id=3, has_side_effects=True, vmem_limit_bytes=60 * 1024 * 1024
+            collective_id=3, has_side_effects=True, vmem_limit_bytes=24 * 1024 * 1024
         ),
         name="reduce_and_swap",
     )(parts, first, second)
@@ -399,7 +399,7 @@
         in_specs=[VMEM] * len(operands),
         out_specs=[VMEM] * len(outs),
         scratch_shapes=scratch,
-        compiler_params=pltpu.CompilerParams(vmem_limit_bytes=60 * 1024 * 1024),
+        compiler_params=pltpu.CompilerParams(vmem_limit_bytes=32 * 1024 * 1024),
         name=name,
     )(*operands)
 

time: 128 us -> 121 us (0.945)
  Pallas kernels: 97.5 us -> 88 us
  local copies, waits for them, and re-layouts: 24.1 us -> 29.5 us
  other arithmetic: 4.47 us -> 2.03 us
    unnamed x10 -> x46, local copies, waits for them, and re-layouts: 1.05 us -> 12.1 us
    pallas_call x3, Pallas kernels: 20.3 us -> 13.4 us  [single(): pl.pallas_call(body, out_shape=outs, in_specs=[VMEM] * len(operands), out...]
    pallas_call x1, Pallas kernels: 37.2 us -> 34.6 us  [reduce_and_swap(): pl.pallas_call(functools.partial(reduce_kernel, count_y, count_z, chains)...]
    reshape x4, local copies, waits for them, and re-layouts: 3.55 us -> 2.13 us  [to_lines(): swapped.reshape(-1, planes, part_y, part_z, width).transpose(1, 3, 0, 2, 4)]
where the time goes in v4:
time: 121 us
  Pallas kernels  88 us (73%)
  local copies, waits for them, and re-layouts  29.5 us (24%)
  other arithmetic  2.03 us (2%)
    pallas_call x1, Pallas kernels, reduce_and_swap(): pl.pallas_call(functools.partial(reduce_kernel, count_y, count_z, chains)...  34.6 us
    pallas_call x2, Pallas kernels, halo(): pl.pallas_call(functools.partial(halo_kernel, count_y, count_z), out_shap...  23.5 us
    pallas_call x1, Pallas kernels, swap_lines(): pl.pallas_call(functools.partial(swap_kernel, count), out_shape=(shape, s...  16.5 us
    pallas_call x3, Pallas kernels, single(): pl.pallas_call(body, out_shape=outs, in_specs=[VMEM] * len(operands), out...  13.4 us
    unnamed x46, local copies, waits for them, and re-layouts  12.1 us

profile of v4, /device:TPU:0, one launch (start us, length us, event | category | flops | bytes accessed | tf_op | source)
XLA Modules:
  0.0 120.6 jit_solution(6622210248667232156)
XLA Ops:
  2.1 0.8 rev.3
  3.2 1.9 %reshape.97.first_in = bf16[8,64,192]{2,1,0:T(8,128)(2,1)} reshape(bf16[16,8,4,192]{3,2,1,0:T(4,128)(2,1)} %param.8) | data formatting | bytes 393216 | tf_op jit(solution)/shard_map/reshape | solution.py:612
  5.1 1.9 %reshape.98.second_in = bf16[8,64,192]{2,1,0:T(8,128)(2,1)} reshape(bf16[16,8,4,192]{3,2,1,0:T(4,128)(2,1)} %param.15) | data formatting | bytes 393216 | tf_op jit(solution)/shard_map/reshape | solution.py:612
  6.9 16.5 %swap_lines.1 = (bf16[8,64,192]{2,1,0:T(8,128)(2,1)}, bf16[8,64,192]{2,1,0:T(8,128)(2,1)}) custom-call(bf16[8,64,192]{2,1,0:T(8,128)(2,1)} %reshape.97.first_in, bf16[8,64,192]{2,1,0:T(8,128)(2,1)} %reshape.98.second_in), custom_call_target="tpu_custom_call" | custom-call | tf_op jit(solution)/shard_map/swap_lines/pallas_call | solution.py:99
  23.4 1.0 reshape.99
  24.5 1.0 reshape.101
  25.8 2.0 %attention_forward.1 = (bf16[2,4,64,192]{3,2,1,0:T(8,128)(2,1)S(1)}, bf16[512,192]{1,0:T(8,128)(2,1)S(1)}, bf16[512,192]{1,0:T(8,128)(2,1)S(1)}, bf16[512,192]{1,0:T(8,128)(2,1)S(1)}, bf16[512,192]{1,0:T(8,128)(2,1)S(1)}) custom-call(bf16[2,4,64,192]{3,2,1,0:T(8,128)(2,1)S(1)} %bitcast.39, bf16[192,576]{1,0:T(8,128)(2,1)S(1)} %copy-done.3, ...), custom_call_target="tpu_custom_call" | custom-call | tf_op jit(solution)/shard_map/attention_forward/pallas_call | solution.py:396
  31.3 13.5 %halo1.1.padded.padded_value = bf16[4,6,64,192]{3,2,1,0:T(8,128)(2,1)} custom-call(bf16[2,4,64,192]{3,2,1,0:T(8,128)(2,1)} %copy-done.12), custom_call_target="tpu_custom_call" | custom-call | tf_op jit(solution)/shard_map/halo1/pallas_call | solution.py:179
  44.9 1.1 copy-done
  46.0 1.0 copy-done.7
  47.0 3.6 %feed_forward.1 = (bf16[2,4,64,192]{3,2,1,0:T(8,128)(2,1)S(1)}, bf16[2,4,64,192]{3,2,1,0:T(8,128)(2,1)S(1)}, f32[72,16,128]{2,1,0:T(8,128)S(1)}, f32[72,16,128]{2,1,0:T(8,128)S(1)}) custom-call(bf16[4,6,64,192]{3,2,1,0:T(8,128)(2,1)S(1)} %copy-done, bf16[2,4,64,192]{3,2,1,0:T(8,128)(2,1)S(1)} %bitcast.43, f32[27,192]{1,0:T(8,128)S(1)} %reshape.103.taps, ...), custom_call_target="tpu_custom_call" | custom-call | tf_op jit(solution)/shard_map/feed_forward/pallas_call | solution.py:396
  50.6 0.9 copy.43
  51.5 1.1 reshape.108.first_in
  52.6 10.0 %halo2.1.padded_grad = bf16[4,6,64,192]{3,2,1,0:T(8,128)(2,1)} custom-call(bf16[2,4,64,192]{3,2,1,0:T(8,128)(2,1)} %copy-done.11), custom_call_target="tpu_custom_call" | custom-call | tf_op jit(solution)/shard_map/halo2/pallas_call | solution.py:179
  62.6 1.1 copy-done.2
  63.8 0.9 copy-done.16
  64.7 0.9 copy-done.18
  65.7 0.9 copy-done.20
  66.6 7.8 %attention_backward.1 = (bf16[2,4,64,192]{3,2,1,0:T(8,128)(2,1)S(1)}, f32[72,16,128]{2,1,0:T(8,128)S(1)}, f32[27,192]{1,0:T(8,128)S(1)}) custom-call(bf16[4,6,64,192]{3,2,1,0:T(8,128)(2,1)S(1)} %copy-done.1, bf16[4,6,64,192]{3,2,1,0:T(8,128)(2,1)S(1)} %copy-done.2, bf16[2,4,64,192]{3,2,1,0:T(8,128)(2,1)S(1)} %bitcast.40, bf16[512,192]{1,0:T(8,128)(2,1)S(1)} %copy-done.14, ...), custom_call_target="tpu_custom_call" | custom-call | tf_op jit(solution)/shard_map/attention_backward/pallas_call | solution.py:396
  76.1 1.2 %pad_maximum_fusion.parts = f32[224,16,128]{2,1,0:T(8,128)S(1)} fusion(f32[8,16,128]{2,1,0:T(8,128)S(1)} %bitcast.56, f32[72,16,128]{2,1,0:T(8,128)} %copy-done.4, f32[72,16,128]{2,1,0:T(8,128)S(1)} %get-tuple-element.28, f32[72,16,128]{2,1,0:T(8,128)S(1)} %get-tuple-element.27), kind=kLoop, calls=%fused_computation | loop fusion | flops 1376256 | bytes 3670016 | tf_op jit(solution)/shard_map/concatenate | solution.py:633
  77.7 34.6 %reduce_and_swap.1 = (bf16[224,16,128]{2,1,0:T(8,128)(2,1)S(1)}, bf16[8,64,192]{2,1,0:T(8,128)(2,1)S(1)}, bf16[8,64,192]{2,1,0:T(8,128)(2,1)S(1)}) custom-call(f32[224,16,128]{2,1,0:T(8,128)S(1)} %pad_maximum_fusion.parts, bf16[8,64,192]{2,1,0:T(8,128)(2,1)S(1)} %reshape.108.first_in, bf16[8,64,192]{2,1,0:T(8,128)(2,1)S(1)} %reshape.110.second_in), custom_call_target="tpu_custom_call" | custom-call | tf_op jit(solution)/shard_map/reduce_and_swap/pallas_call | solution.py:303
  113.0 1.7 %reshape.111 = bf16[16,8,4,192]{3,2,1,0:T(4,128)(2,1)} reshape(bf16[8,64,192]{2,1,0:T(8,128)(2,1)} %copy-done.10) | data formatting | bytes 393216 | tf_op jit(solution)/shard_map/reshape | solution.py:645
  117.2 1.3 %bitcast_bitcast_fusion = (f32[768,192]{0,1:T(8,128)}, f32[192,768]{1,0:T(8,128)}) fusion(f32[24,8,6,128]{3,2,1,0:T(8,128)S(1)} %bitcast.47, f32[24,8,6,128]{3,2,1,0:T(8,128)S(1)} %bitcast.46), kind=kLoop, calls=%fused_computation.2 | loop fusion | bytes 2359296 | tf_op jit(solution)/shard_map/transpose | solution.py:641
  119.8 0.8 slice.29
  (62 shorter events, 11.9 us)
Async XLA Ops:
  3.2 22.4 %copy-start.21 = (bf16[768,192]{0,1:T(8,128)(2,1)S(1)}, bf16[768,192]{0,1:T(8,128)(2,1)}, u32[]{:S(2)}) copy-start(bf16[768,192]{0,1:T(8,128)(2,1)} %param.13) | copy-start | bytes 884740
  5.0 20.7 %copy-start.3 = (bf16[192,576]{1,0:T(8,128)(2,1)S(1)}, bf16[192,576]{1,0:T(8,128)(2,1)}, u32[]{:S(2)}) copy-start(bf16[192,576]{1,0:T(8,128)(2,1)} %qkv_weight.3) | copy-start | bytes 663556
  5.1 20.7 %copy-start.5 = (bf16[192,192]{1,0:T(8,128)(2,1)S(1)}, bf16[192,192]{1,0:T(8,128)(2,1)}, u32[]{:S(2)}) copy-start(bf16[192,192]{1,0:T(8,128)(2,1)} %out_weight.3) | copy-start | bytes 221188
  27.8 0.7 copy-start.12
  28.5 0.7 copy-start.13
  29.2 0.7 copy-start.15
  29.9 0.7 copy-start.17
  30.6 0.7 copy-start.19
  44.9 1.1 copy-start
  46.0 1.0 copy-start.7
  47.0 15.7 %copy-start.1 = (bf16[4,6,64,192]{3,2,1,0:T(8,128)(2,1)S(1)}, bf16[4,6,64,192]{3,2,1,0:T(8,128)(2,1)}, u32[]{:S(2)}) copy-start(bf16[4,6,64,192]{3,2,1,0:T(8,128)(2,1)} %halo1.1.padded.padded_value) | copy-start | bytes 1769476
  50.6 1.0 copy-start.11
  50.6 12.0 %copy-start.6 = (bf16[192,192]{1,0:T(8,128)(2,1)S(1)}, bf16[192,192]{1,0:T(8,128)(2,1)}, u32[]{:S(2)}) copy-start(bf16[192,192]{1,0:T(8,128)(2,1)} %out_weight.3) | copy-start | bytes 221188
  50.6 12.0 %copy-start.14 = (bf16[512,192]{1,0:T(8,128)(2,1)S(1)}, bf16[512,192]{1,0:T(8,128)(2,1)}, u32[]{:S(2)}) copy-start(bf16[512,192]{1,0:T(8,128)(2,1)} %copy-done.13) | copy-start | bytes 589828
  62.6 1.1 copy-start.2
  63.8 0.9 copy-start.16
  64.7 0.9 copy-start.18
  65.7 0.9 copy-start.20
  74.5 0.8 copy-start.4
  75.3 0.7 copy-start.8
  76.1 1.2 %copy-start.9 = (bf16[2,4,64,192]{3,2,1,0:T(8,128)(2,1)S(1)}, bf16[2,4,64,192]{3,2,1,0:T(8,128)(2,1)}, u32[]{:S(2)}) copy-start(bf16[2,4,64,192]{3,2,1,0:T(8,128)(2,1)} %copy-done.8) | copy-start | bytes 589828
  112.3 0.7 copy-start.10
